TPU v7x, 32 devices: a whole 2x2x4 slice. The times are simulated.
32 devices in a mesh: grp: 4 (over x, core), seq: 8 (over z, y).
Axes of the slice: x: 2, y: 2, z: 4, core: 2. Of those that a mesh axis runs over, the one named last changes fastest.
Arguments:
- tile_cls: bfloat16 [8192, 1536], P(('grp', 'seq')), may hold values from -6 to 6
- ln_gain: float32 [1536], replicated, may hold values from 0.25 to 1.75
- ln_bias: float32 [1536], replicated, may hold values from -1.5 to 1.5
- gate_weight: bfloat16 [4096, 1536], P('seq'), may hold values from -0.15625 to 0.15625
- up_weight: bfloat16 [4096, 1536], P('seq'), may hold values from -0.15625 to 0.15625
- down_weight: bfloat16 [4096, 1536], P('seq'), may hold values from -0.09375 to 0.09375
- layer_scale: float32 [1536], replicated, may hold values from 0.25 to 1.75
- final_gain: float32 [1536], replicated, may hold values from 0.25 to 1.75
- final_bias: float32 [1536], replicated, may hold values from -1.5 to 1.5
- proj_weight: bfloat16 [1536, 768], replicated, may hold values from -0.15625 to 0.15625
- proj_bias: float32 [768], replicated, may hold values from -1.5 to 1.5
- slot: int32 [8192], P(('grp', 'seq')), may hold values from 0 to 8191, as said below
- slide_lengths: int32 [4, 4], P('grp'), may hold values from 1 to 1024, 2048 in all within a row
- attn_gain: float32 [768], replicated, may hold values from 0.25 to 1.75
- attn_bias: float32 [768], replicated, may hold values from -1.5 to 1.5
- q_weight: bfloat16 [768, 768], replicated
- k_weight: bfloat16 [768, 768], replicated
- v_weight: bfloat16 [768, 768], replicated, may hold values from -0.21875 to 0.21875
- o_weight: bfloat16 [768, 768], replicated, may hold values from -0.21875 to 0.21875
Outputs:
- slide_out: bfloat16 [4, 2048, 768], P('grp', 'seq')
Inputs may be any that keep to these rules, and one draw needn't show every extreme that they name: slot is a permutation of all tile positions; tile t goes to device slot[t] // 256 (grp major, then seq), row slot[t] % 256; at most 16 tiles of one device go to one device, and that count is reached. `slide_lengths`: each group's lengths add up to 2048.
All inputs are finite; a program needn't handle non-finite values.
Results may differ from a plain program's by a relative error of at most 0.014.
Values may be sent and summed in bfloat16 or wider, within the bound.
A program may use at most 128 MiB of HBM per device.

v0:
```python
import jax
import jax.numpy as jnp
from jax import lax
from jax.sharding import PartitionSpec as P

HEADS = 12
HEAD_DIM = 64
W_SEG = 1024
RATE = 16


def swapped(block, axis, bit):
    count = lax.axis_size(axis)
    route = []
    for low in range(count):
        high = low | 1 << bit
        if high != low and high < count:
            route += [(low, high), (high, low)]
    return lax.ppermute(block, axis, route)


def layer_norm(values, gain_vec, bias_vector):
    average = jnp.mean(values, -1, keepdims=True)
    centred = values - average
    variance = jnp.mean(centred * centred, -1, keepdims=True)
    return centred * lax.rsqrt(variance + 1e-06) * gain_vec + bias_vector


def swiglu_term(normed_rows, gate_rows, up_rows, down_rows):
    dims = (((1,), (1,)), ((), ()))
    gate = lax.dot_general(normed_rows, gate_rows, dims, preferred_element_type=jnp.float32)
    up_part = lax.dot_general(normed_rows, up_rows, dims, preferred_element_type=jnp.float32)
    hidden = (jax.nn.silu(gate) * up_part).astype(jnp.bfloat16)
    return jnp.dot(hidden, down_rows, preferred_element_type=jnp.float32)


def pick_dilated(array, picked):
    grid = array.reshape(picked, RATE, HEADS, HEAD_DIM)[:, :HEADS]
    return jnp.transpose(jnp.diagonal(grid, axis1=1, axis2=2), (0, 2, 1))


def combine(local_out, local_lse, far_out, far_lse, length):
    picked = length // RATE
    chosen = jnp.tile(jnp.arange(RATE)[:, None] == jnp.arange(HEADS)[None, :], (picked, 1))
    distant_output_total = jnp.broadcast_to(
        jnp.transpose(far_out, (1, 0, 2))[:, None], (picked, RATE, HEADS, HEAD_DIM)
    ).reshape(length, HEADS, HEAD_DIM)
    distant_logsumexp_total = jnp.broadcast_to(
        jnp.transpose(far_lse)[:, None], (picked, RATE, HEADS)
    ).reshape(length, HEADS)
    peak = jnp.where(chosen, jnp.maximum(local_lse, distant_logsumexp_total), local_lse)
    local_share = jnp.exp(local_lse - peak)
    far_share = jnp.where(chosen, jnp.exp(distant_logsumexp_total - peak), 0.0)
    mixed = (local_share[..., None] * local_out + far_share[..., None] * distant_output_total) / (
        local_share + far_share
    )[..., None]
    return mixed.reshape(length, HEADS * HEAD_DIM)


def local(
    tile_cls,
    ln_gain,
    ln_bias,
    gate_weight,
    up_weight,
    down_weight,
    layer_scale,
    final_gain,
    final_bias,
    proj_weight,
    proj_bias,
    slot,
    slide_lengths,
    attn_gain,
    attn_bias,
    q_weight,
    k_weight,
    v_weight,
    o_weight,
):
    tile_rows = tile_cls.shape[0]
    width = proj_weight.shape[1]
    residual = tile_cls.astype(jnp.float32)
    normed = layer_norm(residual, ln_gain, ln_bias).astype(jnp.bfloat16)
    gathered = lax.all_gather(normed, "seq", axis=0, tiled=True)
    mlp_out = lax.psum_scatter(
        swiglu_term(gathered, gate_weight, up_weight, down_weight),
        "seq",
        scatter_dimension=0,
        tiled=True,
    )
    tile_out = residual + layer_scale * mlp_out
    final = layer_norm(tile_out, final_gain, final_bias).astype(jnp.bfloat16)
    embed = (jnp.dot(final, proj_weight, preferred_element_type=jnp.float32) + proj_bias).astype(
        jnp.bfloat16
    )
    devices = lax.axis_size("grp") * lax.axis_size("seq")
    capacity = 2 * tile_rows // devices
    target = slot // tile_rows
    position = slot % tile_rows
    onehot = (target[:, None] == jnp.arange(devices, dtype=jnp.int32)[None, :]).astype(jnp.int32)
    bucket_rank = jnp.sum((jnp.cumsum(onehot, 0) - onehot) * onehot, 1)
    outgoing = (
        jnp.zeros((devices, capacity, width), jnp.bfloat16).at[target, bucket_rank].set(embed)
    )
    outgoing_place = (
        jnp.full((devices, capacity), tile_rows, jnp.int32).at[target, bucket_rank].set(position)
    )
    incoming, incoming_place = (
        lax.all_to_all(outgoing, ("grp", "seq"), split_axis=0, concat_axis=0, tiled=True),
        lax.all_to_all(outgoing_place, ("grp", "seq"), split_axis=0, concat_axis=0, tiled=True),
    )
    arrived = incoming.reshape(-1, width)
    arrived_place = incoming_place.reshape(-1)
    placed = jnp.zeros((tile_rows, width), jnp.bfloat16).at[arrived_place].set(arrived, mode="drop")
    seq_index = lax.axis_index("seq")
    start_pos = seq_index * tile_rows
    slide_ends = jnp.cumsum(slide_lengths[0])

    def slides_from(first_pos, count):
        spots = first_pos + jnp.arange(count, dtype=jnp.int32)
        return jnp.sum((spots[:, None] >= slide_ends[None, :]).astype(jnp.int32), 1)

    slide_of = slides_from(start_pos, tile_rows)
    seq_resid = placed.astype(jnp.float32)
    normed_seq = layer_norm(seq_resid, attn_gain, attn_bias).astype(jnp.bfloat16)
    queries = jnp.dot(normed_seq, q_weight, preferred_element_type=jnp.float32).astype(jnp.bfloat16)
    keys_proj = jnp.dot(normed_seq, k_weight, preferred_element_type=jnp.float32).astype(
        jnp.bfloat16
    )
    values_proj = jnp.dot(normed_seq, v_weight, preferred_element_type=jnp.float32).astype(
        jnp.bfloat16
    )
    scale_factor = HEAD_DIM ** (-0.5)
    span = W_SEG // tile_rows
    levels = span.bit_length() - 1
    head_q = queries.reshape(tile_rows, HEADS, HEAD_DIM)
    block_first = seq_index // span * span
    collected_keys = keys_proj
    collected_values = values_proj
    piece_list = [(keys_proj, values_proj, seq_index, 1)]
    for bit in range(levels):
        step_size = 1 << bit
        other_keys, other_values = swapped((collected_keys, collected_values), "seq", bit)
        bit_value = seq_index // step_size % 2
        partner_first = (seq_index // step_size + 1 - 2 * bit_value) * step_size
        piece_list.append((other_keys, other_values, partner_first, step_size))
        is_upper = bit_value == 1
        collected_keys = jnp.where(
            is_upper,
            jnp.concatenate([other_keys, collected_keys], 0),
            jnp.concatenate([collected_keys, other_keys], 0),
        )
        collected_values = jnp.where(
            is_upper,
            jnp.concatenate([other_values, collected_values], 0),
            jnp.concatenate([collected_values, other_values], 0),
        )
    key_total = span * tile_rows
    all_keys = collected_keys.reshape(key_total, HEADS, HEAD_DIM)
    all_values = collected_values.reshape(key_total, HEADS, HEAD_DIM)
    all_mask = (slide_of[:, None] == slides_from(block_first * tile_rows, key_total)[None, :])[None]
    scores = (
        jnp.einsum("qhd,khd->hqk", head_q, all_keys, preferred_element_type=jnp.float32)
        * scale_factor
    )
    row_max = jnp.max(jnp.where(all_mask, scores, -1e30), -1, keepdims=True)
    weights = jnp.where(all_mask, jnp.exp(scores - row_max), 0.0)
    denom_sum = jnp.sum(weights, -1)
    mixed = (
        jnp.einsum(
            "hqk,khd->hqd",
            weights.astype(jnp.bfloat16),
            all_values,
            preferred_element_type=jnp.float32,
        )
        / denom_sum[..., None]
    )
    block_lse = row_max[..., 0] + jnp.log(denom_sum)
    local_out = jnp.transpose(mixed, (1, 0, 2))
    local_lse = jnp.transpose(block_lse)
    picked = tile_rows // RATE
    selected_query = pick_dilated(queries, picked)
    chosen_k = pick_dilated(keys_proj, picked).reshape(picked, width)
    chosen_v = pick_dilated(values_proj, picked).reshape(picked, width)
    query_slide = jnp.transpose(slide_of.reshape(picked, RATE)[:, :HEADS])
    all_keys, all_values = (
        lax.all_gather(chosen_k, "seq", axis=0, tiled=True),
        lax.all_gather(chosen_v, "seq", axis=0, tiled=True),
    )
    key_count = all_keys.shape[0]
    key_head_rows = all_keys.reshape(key_count, HEADS, HEAD_DIM)
    value_heads = all_values.reshape(key_count, HEADS, HEAD_DIM)
    far_scores = (
        jnp.einsum(
            "tbx,pbx->btp", selected_query, key_head_rows, preferred_element_type=jnp.float32
        )
        * scale_factor
    )
    key_pos = (
        jnp.arange(key_count, dtype=jnp.int32)[None, :] * RATE
        + jnp.arange(HEADS, dtype=jnp.int32)[:, None]
    )
    far_allowed = (
        query_slide[:, :, None]
        == jnp.sum((key_pos[..., None] >= slide_ends[None, None, :]).astype(jnp.int32), -1)[
            :, None, :
        ]
    )
    far_max = jnp.max(jnp.where(far_allowed, far_scores, -1e30), -1, keepdims=True)
    far_weights = jnp.where(far_allowed, jnp.exp(far_scores - far_max), 0.0)
    far_sum = jnp.sum(far_weights, -1)
    far_out = (
        jnp.einsum(
            "gbr,rga->gba",
            far_weights.astype(jnp.bfloat16),
            value_heads,
            preferred_element_type=jnp.float32,
        )
        / far_sum[..., None]
    )
    far_lse = far_max[..., 0] + jnp.log(far_sum)
    attn = combine(local_out, local_lse, far_out, far_lse, tile_rows).astype(jnp.bfloat16)
    result = (seq_resid + jnp.dot(attn, o_weight, preferred_element_type=jnp.float32)).astype(
        jnp.bfloat16
    )
    return result[None]


def solution(mesh):
    return jax.shard_map(
        local,
        mesh=mesh,
        in_specs=(
            P(("grp", "seq"), None),
            P(),
            P(),
            P("seq", None),
            P("seq", None),
            P("seq", None),
            P(),
            P(),
            P(),
            P(),
            P(),
            P(("grp", "seq")),
            P("grp", None),
            P(),
            P(),
            P(),
            P(),
            P(),
            P(),
        ),
        out_specs=P("grp", "seq", None),
        check_vma=False,
    )
```

profile of v0, /device:TPU:0, one launch (start us, length us, event | category | flops | bytes accessed | tf_op | source)
XLA Modules:
  0.0 530.8 jit_solution(18102635890574513353)
XLA Ops:
  6.6 1.5 convert_reduce_fusion
  8.1 1.5 fusion.7
  9.6 1.2 fusion.10
  10.9 101.8 %all-gather.2.cloned.1.call-done = bf16[2048,1536]{1,0:T(8,128)(2,1)} async-done(((bf16[256,1536]{1,0:T(8,128)(2,1)}), bf16[2048,1536]{1,0:T(8,128)(2,1)}) %all-gather.2.cloned.1.call-update) | async-done | bytes 6291472 | tf_op jit(solution)/shard_map/all_gather | solution.py:85
  112.7 8.7 %fusion.91 = f32[2048,512]{1,0:T(8,128)} fusion(bf16[2048,1536]{1,0:T(8,128)(2,1)} %all-gather.2.cloned.1.call-done, bf16[512,1536]{1,0:T(8,128)(2,1)} %param.22), kind=kOutput, calls=%fused_computation.144 | convolution fusion | flops 3221225472 | bytes 12058624 | tf_op jit(solution)/shard_map/dot_general | solution.py:31
  121.5 13.1 %fusion.31 = f32[2048,1536]{1,0:T(8,128)} fusion(bf16[512,1536]{1,0:T(8,128)(2,1)} %param.24, f32[2048,512]{1,0:T(8,128)} %fusion.91, bf16[2048,1536]{1,0:T(8,128)(2,1)} %all-gather.2.cloned.1.call-done, bf16[512,1536]{1,0:T(8,128)(2,1)} %param.23), kind=kOutput, calls=%fused_computation.53 | convolution fusion | flops 6448742400 | bytes 26214400 | tf_op jit(solution)/shard_map/dot_general | solution.py:34
  134.6 0.7 copy-done.24
  135.3 0.6 reduce-window.18
  136.3 12.8 %scatter_fusion = s32[32,16]{0,1:T(8,128)S(1)} fusion(s32[32,16]{0,1:T(8,128)S(1)} %broadcast_in_dim.50, s32[256]{0:T(256)S(1)} %bitcast.113, s32[256]{0:T(256)S(1)} %get-tuple-element.10), kind=kCustom, calls=%fused_computation.3 | custom fusion | bytes 5120 | tf_op jit(solution)/shard_map/scatter | solution.py:107
  149.0 0.7 copy.73
  149.7 3.2 all-to-all-start
  153.2 0.7 reshape.280
  153.9 187.2 %reduce-scatter.2.cloned.1.call-done = f32[256,1536]{1,0:T(8,128)} async-done(((f32[2048,1536]{1,0:T(8,128)}), f32[256,1536]{1,0:T(8,128)}) %reduce-scatter.2.cloned.1.call-update) | async-done | bytes 1572880 | tf_op jit(solution)/shard_map/reduce_scatter | solution.py:86
  341.1 1.8 fusion.57
  343.6 1.0 fusion.27
  344.7 0.9 broadcast_in_dim.53
  345.6 34.3 %scatter_fusion.1 = bf16[32,16,768]{2,1,0:T(8,128)(2,1)} fusion(bf16[32,16,768]{2,1,0:T(8,128)(2,1)} %broadcast_in_dim.53, s32[256]{0:T(256)S(1)} %bitcast.114, bf16[256,768]{1,0:T(8,128)(2,1)S(1)} %fusion.27), kind=kCustom, calls=%fused_computation.4 | custom fusion | bytes 1181696 | tf_op jit(solution)/shard_map/scatter | solution.py:104
  379.9 3.8 all-to-all-start.1
  384.2 0.9 broadcast_compare_fusion
  385.7 1.4 reduce.5
  387.2 18.3 %all-to-all-done.1 = bf16[32,16,768]{2,1,0:T(8,128)(2,1)S(1)} async-done(((bf16[32,16,768]{2,1,0:T(8,128)(2,1)}), bf16[32,16,768]{2,1,0:T(8,128)(2,1)S(1)}, u32[]{:S(2)}, u32[]{:S(2)}) %all-to-all-start.1) | async-done | bytes 786464 | tf_op jit(solution)/shard_map/all_to_all | solution.py:110
  405.5 2.7 scatter_custom_fusion.2
  408.7 0.6 convolution_convert_fusion.1
  409.2 0.8 collective-permute-start
  410.1 0.6 reshape.282
  410.7 1.9 convolution_convert_fusion.2
  413.2 1.3 collective-permute-start.2
  415.1 0.6 gather_fusion.1
  415.8 36.9 %all_gather.10 = bf16[128,768]{1,0:T(8,128)(2,1)S(1)} all-gather(bf16[16,768]{1,0:T(8,128)(2,1)S(1)} %reshape.283), channel_id=1, replica_groups=mesh['grp'=4,'seq'=8] {'seq'}, dimensions={0}, use_global_device_ids=true | all-gather | bytes 221184 | tf_op jit(solution)/shard_map/all_gather | solution.py:188
  452.7 0.6 reshape.281
  453.9 0.6 gather_fusion
  455.2 1.2 maximum_select_fusion.16
  456.4 0.9 copy.74
  457.5 0.9 copy.77
  458.4 0.6 reshape.286
  459.1 0.7 reshape.285
  460.4 0.6 gather_fusion.2
  461.2 33.3 %all_gather.11 = bf16[128,768]{1,0:T(8,128)(2,1)S(1)} all-gather(bf16[16,768]{1,0:T(8,128)(2,1)S(1)} %reshape.287), channel_id=1, replica_groups=mesh['grp'=4,'seq'=8] {'seq'}, dimensions={0}, use_global_device_ids=true | all-gather | bytes 221184 | tf_op jit(solution)/shard_map/all_gather | solution.py:189
  495.1 1.4 copy.89
  496.5 1.4 maximum_select_fusion.18
  498.0 1.2 copy.84
  499.3 1.7 maximum_select_fusion.17
  501.0 1.5 copy.75
  502.5 4.2 select_reduce_fusion
  506.7 4.0 fusion.1
  511.3 2.3 copy.83
  513.6 9.1 %fusion.44 = bf16[256,12,64]{0,2,1:T(8,128)(2,1)S(1)} fusion(bf16[512,12,64]{0,2,1:T(8,128)(2,1)} %get-tuple-element.16, bf16[512,12,64]{0,2,1:T(8,128)(2,1)} %bitcast.126, pred[]{:T(512)S(6)} %eq.97, f32[12,256,1024]{2,1,0:T(8,128)} %copy-done.3, f32[12,256]{1,0:T(8,128)S(1)} %get-tuple-element.11, pred[256,1024]{1,0:T(8,128)(4,1)S(1)} %copy-done.7, ...), kind=kOutput, calls=%fused_computation.58 | convolution fusion | flops 423493632 | bytes 15659009 | tf_op jit(solution)/shard_map/hqk,khd->hqd/dot_general | solution.py:171
  522.7 1.3 fusion.29
  (132 shorter events, 7.6 us)
Async XLA Ops:
  6.5 336.9 %copy-start = (bf16[1536,768]{1,0:T(8,128)(2,1)S(1)}, bf16[1536,768]{1,0:T(8,128)(2,1)}, u32[]{:S(2)}) copy-start(bf16[1536,768]{1,0:T(8,128)(2,1)} %param.28) | copy-start | bytes 7077892
  6.5 3.0 copy-start.2
  6.5 3.0 copy-start.21
  6.5 3.0 copy-start.20
  6.5 106.2 %all-gather.2.cloned.1.call-start = ((), (), s32[]{:S(2)}) async-start(), calls=%async_computation.3 | async-start | bytes 7077888 | tf_op jit(solution)/shard_map/all_gather | solution.py:85
  10.9 330.3 %reduce-scatter.2.cloned.1.call-start = ((), (), s32[]{:S(2)}) async-start(), calls=%async_computation.4 | async-start | bytes 14155776 | tf_op jit(solution)/shard_map/reduce_scatter | solution.py:86
  134.6 0.7 copy-start.24
  135.3 17.7 %copy-start.32 = (s32[1,4]{1,0:T(1,128)S(1)}, s32[1,4]{1,0:T(1,128)}, u32[]{:S(2)}) copy-start(s32[1,4]{1,0:T(1,128)} %param.31) | copy-start | bytes 52
  135.3 205.8 %copy-start.14 = (f32[1536]{0:T(1024)S(1)}, f32[1536]{0:T(1024)}, u32[]{:S(2)}) copy-start(f32[1536]{0:T(1024)} %param.25) | copy-start | bytes 18436
  149.7 230.2 %all-to-all-start = ((s32[32,1,16]{2,1,0:T(1,128)}), s32[32,1,16]{2,1,0:T(1,128)}, u32[]{:S(2)}, u32[]{:S(2)}) async-start(s32[32,1,16]{2,1,0:T(1,128)} %copy.73), calls=%async_computation | async-start | bytes 32768 | tf_op jit(solution)/shard_map/all_to_all | solution.py:111
  153.2 190.3 %copy-start.22 = (s32[4,1]{0,1:T(1,128)}, s32[4,1]{0,1:T(1,128)S(1)}, u32[]{:S(2)}) copy-start(s32[4,1]{0,1:T(1,128)S(1)} %reduce-window.20) | copy-start | bytes 52
  153.2 190.2 %copy-start.18 = (s32[256]{0:T(256)}, s32[256]{0:T(256)S(1)}, u32[]{:S(2)}) copy-start(s32[256]{0:T(256)S(1)} %convert_reduce_fusion.4) | copy-start | bytes 3076
  341.1 1.9 copy-start.4
  342.9 0.7 copy-start.27
  342.9 0.7 copy-start.28
  342.9 0.7 copy-start.29
  379.9 3.9 copy-start.17
  379.9 4.1 copy-start.23
  379.9 4.3 copy-start.19
  379.9 28.8 %copy-start.25 = (bf16[768,768]{1,0:T(8,128)(2,1)S(1)}, bf16[768,768]{1,0:T(8,128)(2,1)}, u32[]{:S(2)}) copy-start(bf16[768,768]{1,0:T(8,128)(2,1)} %param.35) | copy-start | bytes 3538948
  379.9 28.8 %copy-start.30 = (f32[768]{0:T(1024)S(1)}, f32[768]{0:T(1024)}, u32[]{:S(2)}) copy-start(f32[768]{0:T(1024)} %param.33) | copy-start | bytes 9220
  379.9 28.8 %copy-start.31 = (f32[768]{0:T(1024)S(1)}, f32[768]{0:T(1024)}, u32[]{:S(2)}) copy-start(f32[768]{0:T(1024)} %param.32) | copy-start | bytes 9220
  379.9 25.6 %all-to-all-start.1 = ((bf16[32,16,768]{2,1,0:T(8,128)(2,1)}), bf16[32,16,768]{2,1,0:T(8,128)(2,1)S(1)}, u32[]{:S(2)}, u32[]{:S(2)}) async-start(bf16[32,16,768]{2,1,0:T(8,128)(2,1)} %scatter_fusion.1), calls=%async_computation.2 | async-start | bytes 1572864 | tf_op jit(solution)/shard_map/all_to_all | solution.py:110
  384.2 70.7 %copy-start.11 = (s32[12,128]{1,0:T(8,128)}, s32[12,128]{1,0:T(8,128)S(1)}, u32[]{:S(2)}) copy-start(s32[12,128]{1,0:T(8,128)S(1)} %convert_reduce_fusion.2) | copy-start | bytes 18436
  409.2 46.0 %collective-permute-start = (bf16[256,768]{1,0:T(8,128)(2,1)S(1)}, bf16[256,768]{1,0:T(8,128)(2,1)S(1)}, u32[]{:S(2)}, u32[]{:S(2)}) collective-permute-start(bf16[256,768]{1,0:T(8,128)(2,1)S(1)} %convolution_convert_fusion.1), channel_id=1, source_target_pairs={{0,1},{1,0},{2,3},{3,2},{4,5},{5,4},{6,7},{7,6},{8,9},{9,8},{10,11... | collective-permute-start | bytes 1179656 | tf_op jit(solution)/shard_map/ppermute | solution.py:19
  410.7 1.9 copy-start.26
  413.2 83.3 %collective-permute-start.2 = (bf16[256,768]{1,0:T(8,128)(2,1)S(1)}, bf16[256,768]{1,0:T(8,128)(2,1)}, u32[]{:S(2)}, u32[]{:S(2)}) collective-permute-start(bf16[256,768]{1,0:T(8,128)(2,1)S(1)} %convolution_convert_fusion), channel_id=1, source_target_pairs={{0,1},{1,0},{2,3},{3,2},{4,5},{5,4},{6,7},{7,6},{8,9},{9,8},{10,11... | collective-permute-start | bytes 1179656 | tf_op jit(solution)/shard_map/ppermute | solution.py:19
  455.0 2.5 copy-start.9
  455.2 2.3 copy-start.15
  456.4 44.6 %collective-permute-start.1 = (bf16[512,768]{1,0:T(8,128)(2,1)}, bf16[512,768]{1,0:T(8,128)(2,1)}, u32[]{:S(2)}, u32[]{:S(2)}) collective-permute-start(bf16[512,768]{1,0:T(8,128)(2,1)} %maximum_select_fusion.16), channel_id=1, source_target_pairs={{0,2},{2,0},{1,3},{3,1},{4,6},{6,4},{5,7},{7,5},{8,10},{10,8},{9,1... | collective-permute-start | bytes 2359304 | tf_op jit(solution)/shard_map/ppermute | solution.py:19
  460.0 34.7 %copy-start.10 = (f32[12,16,128]{2,1,0:T(8,128)S(1)}, f32[12,16,128]{2,1,0:T(8,128)}, u32[]{:S(2)}) copy-start(f32[12,16,128]{2,1,0:T(8,128)} %copy-done.9) | copy-start | bytes 294916
  460.0 34.7 %copy-start.12 = (s32[12,128]{1,0:T(8,128)S(1)}, s32[12,128]{1,0:T(8,128)}, u32[]{:S(2)}) copy-start(s32[12,128]{1,0:T(8,128)} %copy-done.11) | copy-start | bytes 18436
  460.0 34.7 %copy-start.16 = (f32[12,16]{1,0:T(8,128)S(1)}, f32[12,16]{1,0:T(8,128)}, u32[]{:S(2)}) copy-start(f32[12,16]{1,0:T(8,128)} %copy-done.15) | copy-start | bytes 2308
  496.5 2.8 copy-start.5
  497.9 13.4 %collective-permute-start.3 = (bf16[512,768]{1,0:T(8,128)(2,1)S(1)}, bf16[512,768]{1,0:T(8,128)(2,1)}, u32[]{:S(2)}, u32[]{:S(2)}) collective-permute-start(bf16[512,768]{1,0:T(8,128)(2,1)S(1)} %maximum_select_fusion.18), channel_id=1, source_target_pairs={{0,2},{2,0},{1,3},{3,1},{4,6},{6,4},{5,7},{7,5},{8,10},{10,8},{9,1... | collective-permute-start | bytes 2359304 | tf_op jit(solution)/shard_map/ppermute | solution.py:19
  501.0 1.5 copy-start.7
  501.0 1.5 copy-start.8
  506.7 4.6 copy-start.3
  506.7 4.6 copy-start.13
  513.6 9.1 %copy-start.6 = (bf16[768,768]{1,0:T(8,128)(2,1)S(1)}, bf16[768,768]{1,0:T(8,128)(2,1)}, u32[]{:S(2)}) copy-start(bf16[768,768]{1,0:T(8,128)(2,1)} %param.37) | copy-start | bytes 3538948
  513.6 10.4 %copy-start.1 = (bf16[1536,768]{1,0:T(8,128)(2,1)S(1)}, bf16[1536,768]{1,0:T(8,128)(2,1)}, u32[]{:S(2)}) copy-start(bf16[1536,768]{1,0:T(8,128)(2,1)} %param.28) | copy-start | bytes 7077892
Sparse Core Ops, SparseCore 0:
  11.0 101.7 all-gather.1
  134.7 206.3 reduce-scatter.1
where the time goes:
time: 533 us; the launch traced here: 531 us
  waiting for transfers between devices  307 us (58%)
  blocking collectives  70.2 us (13%)
  local copies, waits for them, and re-layouts  69.8 us (13%)
  matrix products  41 us (8%)
  other arithmetic  18.9 us (4%)
  between operations  14.2 us (3%)
  starting transfers between devices  9.32 us (2%)
    reduce_scatter x1, waiting for transfers between devices, local(): lax.psum_scatter(swiglu_term(gathered, gate_weight, up_weight, down_weigh...  187 us
    all_gather x1, waiting for transfers between devices, local(): gathered = lax.all_gather(normed, 'seq', axis=0, tiled=True)  102 us
    all_gather x1, blocking collectives, local(): lax.all_gather(chosen_k, 'seq', axis=0, tiled=True)  36.9 us
    scatter x1, local copies, waits for them, and re-layouts, local(): jnp.zeros((devices, capacity, width), jnp.bfloat16).at[target, bucket_rank]  34.3 us
    all_gather x1, blocking collectives, local(): lax.all_gather(chosen_v, 'seq', axis=0, tiled=True)  33.3 us
    all_to_all x1, waiting for transfers between devices, local(): lax.all_to_all(outgoing, ('grp', 'seq'), split_axis=0, concat_axis=0, til...  18.3 us
    dot_general x1, matrix products, swiglu_term(): return jnp.dot(hidden, down_rows, preferred_element_type=jnp.float32)  13.1 us
    scatter x1, local copies, waits for them, and re-layouts, local(): jnp.full((devices, capacity), tile_rows, jnp.int32).at[target, bucket_rank]  12.8 us
  transfers between devices with their start and end apart: 8, of which 3 were waited for; matrix products, arithmetic and copies ran while one was open for 16% of the time, Pallas kernels for 0%

commit v1 on v0

--- a/solution.py
+++ b/solution.py
@@ -9,14 +9,64 @@
 RATE = 16
 
 
-def swapped(block, axis, bit):
-    count = lax.axis_size(axis)
-    route = []
-    for low in range(count):
-        high = low | 1 << bit
-        if high != low and high < count:
-            route += [(low, high), (high, low)]
-    return lax.ppermute(block, axis, route)
+def crossed(block, offset):
+    count = lax.axis_size("seq")
+    return lax.ppermute(block, "seq", [(low, low ^ offset) for low in range(count)])
+
+
+def z_shape():
+    count = lax.axis_size("seq")
+    depth = min(4, count)
+    return depth, count // depth
+
+
+def z_hop(block, step, senders):
+    _, across = z_shape()
+    route = [(z * across + y, (z + step) * across + y) for z in senders for y in range(across)]
+    return lax.ppermute(block, "seq", route)
+
+
+def z_slots(block, z_index):
+    depth, _ = z_shape()
+    right, left = block, block
+    rights, lefts = {}, {}
+    for k in range(1, depth):
+        right = z_hop(right, 1, range(k - 1, depth - 1))
+        left = z_hop(left, -1, range(1, depth - k + 1))
+        rights[k], lefts[k] = right, left
+    return [block] + [
+        jnp.where(z_index >= k, rights[k], lefts[depth - k]) for k in range(1, depth)
+    ]
+
+
+def z_reduce(parts):
+    depth, _ = z_shape()
+    right = left = None
+    for t in range(1, depth):
+        to_right, to_left = parts[t], parts[depth - t]
+        if right is not None:
+            to_right, to_left = to_right + right, to_left + left
+        right = z_hop(to_right.astype(jnp.bfloat16), 1, range(t)).astype(jnp.float32)
+        left = z_hop(to_left.astype(jnp.bfloat16), -1, range(depth - t, depth)).astype(
+            jnp.float32
+        )
+    return parts[0] if right is None else parts[0] + right + left
+
+
+def y_weights(weights):
+    _, across = z_shape()
+    half = weights[0].shape[0] // 2
+    first = lax.axis_index("grp") % 2 * half
+    twins = [(low, low ^ 1) for low in range(lax.axis_size("grp"))]
+    out = []
+    for weight in weights:
+        mine = lax.dynamic_slice_in_dim(weight, first, half, 0)
+        pieces = []
+        for offset in range(1, across):
+            piece = crossed(mine, offset)
+            pieces += [piece, lax.ppermute(piece, "grp", twins)]
+        out.append(jnp.concatenate(pieces, 0) if pieces else None)
+    return out
 
 
 def layer_norm(values, gain_vec, bias_vector):
@@ -34,9 +84,11 @@
     return jnp.dot(hidden, down_rows, preferred_element_type=jnp.float32)
 
 
-def pick_dilated(array, picked):
-    grid = array.reshape(picked, RATE, HEADS, HEAD_DIM)[:, :HEADS]
-    return jnp.transpose(jnp.diagonal(grid, axis1=1, axis2=2), (0, 2, 1))
+def pick_dilated(array):
+    width = array.shape[1]
+    grid = array.reshape(-1, RATE, width)
+    own = jnp.arange(RATE)[:, None] == jnp.arange(width)[None, :] // HEAD_DIM
+    return jnp.sum(jnp.where(own[None], grid, 0), 1, dtype=jnp.float32).astype(array.dtype)
 
 
 def combine(local_out, local_lse, far_out, far_lse, length):
@@ -82,13 +134,16 @@
     width = proj_weight.shape[1]
     residual = tile_cls.astype(jnp.float32)
     normed = layer_norm(residual, ln_gain, ln_bias).astype(jnp.bfloat16)
-    gathered = lax.all_gather(normed, "seq", axis=0, tiled=True)
-    mlp_out = lax.psum_scatter(
-        swiglu_term(gathered, gate_weight, up_weight, down_weight),
-        "seq",
-        scatter_dimension=0,
-        tiled=True,
-    )
+    seq_index = lax.axis_index("seq")
+    _, across = z_shape()
+    far_gate, far_up, far_down = y_weights((gate_weight, up_weight, down_weight))
+    terms = []
+    for rows in z_slots(normed, seq_index // across):
+        term = swiglu_term(rows, gate_weight, up_weight, down_weight)
+        if across > 1:
+            term = term + swiglu_term(rows, far_gate, far_up, far_down)
+        terms.append(term)
+    mlp_out = z_reduce(terms)
     tile_out = residual + layer_scale * mlp_out
     final = layer_norm(tile_out, final_gain, final_bias).astype(jnp.bfloat16)
     embed = (jnp.dot(final, proj_weight, preferred_element_type=jnp.float32) + proj_bias).astype(
@@ -98,13 +153,18 @@
     capacity = 2 * tile_rows // devices
     target = slot // tile_rows
     position = slot % tile_rows
-    onehot = (target[:, None] == jnp.arange(devices, dtype=jnp.int32)[None, :]).astype(jnp.int32)
-    bucket_rank = jnp.sum((jnp.cumsum(onehot, 0) - onehot) * onehot, 1)
+    order = jnp.arange(tile_rows, dtype=jnp.int32)
+    same = (target[:, None] == target[None, :]) & (order[None, :] < order[:, None])
+    bucket = target * capacity + jnp.sum(same.astype(jnp.int32), 1)
+    places = jnp.arange(devices * capacity, dtype=jnp.int32)
+    sends = places[:, None] == bucket[None, :]
+    outgoing_place = (
+        jnp.sum(jnp.where(sends, position[None, :] - tile_rows, 0), 1) + tile_rows
+    ).reshape(devices, capacity)
     outgoing = (
-        jnp.zeros((devices, capacity, width), jnp.bfloat16).at[target, bucket_rank].set(embed)
-    )
-    outgoing_place = (
-        jnp.full((devices, capacity), tile_rows, jnp.int32).at[target, bucket_rank].set(position)
+        jnp.dot(sends.astype(jnp.bfloat16), embed, preferred_element_type=jnp.float32)
+        .astype(jnp.bfloat16)
+        .reshape(devices, capacity, width)
     )
     incoming, incoming_place = (
         lax.all_to_all(outgoing, ("grp", "seq"), split_axis=0, concat_axis=0, tiled=True),
@@ -112,8 +172,8 @@
     )
     arrived = incoming.reshape(-1, width)
     arrived_place = incoming_place.reshape(-1)
-    placed = jnp.zeros((tile_rows, width), jnp.bfloat16).at[arrived_place].set(arrived, mode="drop")
-    seq_index = lax.axis_index("seq")
+    lands = (order[:, None] == arrived_place[None, :]).astype(jnp.bfloat16)
+    placed = jnp.dot(lands, arrived, preferred_element_type=jnp.float32).astype(jnp.bfloat16)
     start_pos = seq_index * tile_rows
     slide_ends = jnp.cumsum(slide_lengths[0])
 
@@ -123,8 +183,12 @@
 
     slide_of = slides_from(start_pos, tile_rows)
     seq_resid = placed.astype(jnp.float32)
-    normed_seq = layer_norm(seq_resid, attn_gain, attn_bias).astype(jnp.bfloat16)
-    queries = jnp.dot(normed_seq, q_weight, preferred_element_type=jnp.float32).astype(jnp.bfloat16)
+    span = W_SEG // tile_rows
+    block = jnp.concatenate([placed] + [crossed(placed, r) for r in range(1, span)], 0)
+    normed_seq = layer_norm(block.astype(jnp.float32), attn_gain, attn_bias).astype(jnp.bfloat16)
+    queries = jnp.dot(
+        normed_seq[:tile_rows], q_weight, preferred_element_type=jnp.float32
+    ).astype(jnp.bfloat16)
     keys_proj = jnp.dot(normed_seq, k_weight, preferred_element_type=jnp.float32).astype(
         jnp.bfloat16
     )
@@ -132,34 +196,18 @@
         jnp.bfloat16
     )
     scale_factor = HEAD_DIM ** (-0.5)
-    span = W_SEG // tile_rows
-    levels = span.bit_length() - 1
+    chosen = jnp.concatenate([pick_dilated(keys_proj), pick_dilated(values_proj)], 1)
+    far_pieces = [chosen] + [
+        crossed(chosen, r) for r in range(span, lax.axis_size("seq"), span)
+    ]
     head_q = queries.reshape(tile_rows, HEADS, HEAD_DIM)
-    block_first = seq_index // span * span
-    collected_keys = keys_proj
-    collected_values = values_proj
-    piece_list = [(keys_proj, values_proj, seq_index, 1)]
-    for bit in range(levels):
-        step_size = 1 << bit
-        other_keys, other_values = swapped((collected_keys, collected_values), "seq", bit)
-        bit_value = seq_index // step_size % 2
-        partner_first = (seq_index // step_size + 1 - 2 * bit_value) * step_size
-        piece_list.append((other_keys, other_values, partner_first, step_size))
-        is_upper = bit_value == 1
-        collected_keys = jnp.where(
-            is_upper,
-            jnp.concatenate([other_keys, collected_keys], 0),
-            jnp.concatenate([collected_keys, other_keys], 0),
-        )
-        collected_values = jnp.where(
-            is_upper,
-            jnp.concatenate([other_values, collected_values], 0),
-            jnp.concatenate([collected_values, other_values], 0),
-        )
     key_total = span * tile_rows
-    all_keys = collected_keys.reshape(key_total, HEADS, HEAD_DIM)
-    all_values = collected_values.reshape(key_total, HEADS, HEAD_DIM)
-    all_mask = (slide_of[:, None] == slides_from(block_first * tile_rows, key_total)[None, :])[None]
+    all_keys = keys_proj.reshape(key_total, HEADS, HEAD_DIM)
+    all_values = values_proj.reshape(key_total, HEADS, HEAD_DIM)
+    key_slides = jnp.concatenate(
+        [slides_from((seq_index ^ r) * tile_rows, tile_rows) for r in range(span)]
+    )
+    all_mask = (slide_of[:, None] == key_slides[None, :])[None]
     scores = (
         jnp.einsum("qhd,khd->hqk", head_q, all_keys, preferred_element_type=jnp.float32)
         * scale_factor
@@ -180,27 +228,25 @@
     local_out = jnp.transpose(mixed, (1, 0, 2))
     local_lse = jnp.transpose(block_lse)
     picked = tile_rows // RATE
-    selected_query = pick_dilated(queries, picked)
-    chosen_k = pick_dilated(keys_proj, picked).reshape(picked, width)
-    chosen_v = pick_dilated(values_proj, picked).reshape(picked, width)
+    selected_query = pick_dilated(queries).reshape(picked, HEADS, HEAD_DIM)
     query_slide = jnp.transpose(slide_of.reshape(picked, RATE)[:, :HEADS])
-    all_keys, all_values = (
-        lax.all_gather(chosen_k, "seq", axis=0, tiled=True),
-        lax.all_gather(chosen_v, "seq", axis=0, tiled=True),
-    )
-    key_count = all_keys.shape[0]
-    key_head_rows = all_keys.reshape(key_count, HEADS, HEAD_DIM)
-    value_heads = all_values.reshape(key_count, HEADS, HEAD_DIM)
+    far_rows = jnp.concatenate(far_pieces, 0)
+    key_count = far_rows.shape[0]
+    key_head_rows = far_rows[:, :width].reshape(key_count, HEADS, HEAD_DIM)
+    value_heads = far_rows[:, width:].reshape(key_count, HEADS, HEAD_DIM)
     far_scores = (
         jnp.einsum(
             "tbx,pbx->btp", selected_query, key_head_rows, preferred_element_type=jnp.float32
         )
         * scale_factor
     )
-    key_pos = (
-        jnp.arange(key_count, dtype=jnp.int32)[None, :] * RATE
-        + jnp.arange(HEADS, dtype=jnp.int32)[:, None]
-    )
+    key_first = jnp.concatenate(
+        [
+            (seq_index ^ r) * tile_rows + RATE * jnp.arange(picked, dtype=jnp.int32)
+            for r in range(lax.axis_size("seq"))
+        ]
+    )
+    key_pos = key_first[None, :] + jnp.arange(HEADS, dtype=jnp.int32)[:, None]
     far_allowed = (
         query_slide[:, :, None]
         == jnp.sum((key_pos[..., None] >= slide_ends[None, None, :]).astype(jnp.int32), -1)[

time: 533 us -> 311 us (0.58)
  waiting for transfers between devices: 307 us -> 118 us
  blocking collectives: 70.2 us -> 0 us
  starting transfers between devices: 9.32 us -> 66 us
  local copies, waits for them, and re-layouts: 69.8 us -> 22.7 us
  matrix products: 41 us -> 75.5 us
  between operations: 14.2 us -> 0.75 us
  other arithmetic: 18.9 us -> 26.5 us
    reduce_scatter x1 -> x0, waiting for transfers between devices: 187 us -> none  [local(): lax.psum_scatter(swiglu_term(gathered, gate_weight, up_weight, down_weigh...]
    all_gather x1 -> x0, waiting for transfers between devices: 102 us -> none  [local(): gathered = lax.all_gather(normed, 'seq', axis=0, tiled=True)]
    ppermute x4 -> x22, waiting for transfers between devices: 0.01 us -> 97.8 us  [the longest x12 51.3 us: z_hop(): return lax.ppermute(block, 'seq', route)]
    all_gather x2 -> x0, blocking collectives: 70.2 us -> none  [the longest x1 36.9 us: local(): lax.all_gather(chosen_k, 'seq', axis=0, tiled=True)]
    scatter x3 -> x0, local copies, waits for them, and re-layouts: 49.7 us -> none  [the longest x1 34.3 us: local(): jnp.zeros((devices, capacity, width), jnp.bfloat16).at[target, bucket_rank]]
    ppermute x4 -> x22, starting transfers between devices: 2.23 us -> 36.2 us  [the longest x12 29 us: z_hop(): return lax.ppermute(block, 'seq', route)]
    dot_general x1 -> x8, matrix products: 13.1 us -> 38.4 us  [swiglu_term(): return jnp.dot(hidden, down_rows, preferred_element_type=jnp.float32)]
    all_to_all x1, starting transfers between devices: 3.21 us -> 26.1 us  [local(): lax.all_to_all(outgoing_place, ('grp', 'seq'), split_axis=0, concat_axis=...]
  transfers between devices with their start and end apart: 8 -> 24, of which waited for: 3 -> 12; matrix products, arithmetic and copies ran while one was open for 16% -> 26% of each run, Pallas kernels for 0% -> 0%
where the time goes in v1:
time: 311 us; the launch traced here: 310 us
  waiting for transfers between devices  118 us (38%)
  matrix products  75.5 us (24%)
  starting transfers between devices  66 us (21%)
  other arithmetic  26.5 us (9%)
  local copies, waits for them, and re-layouts  22.7 us (7%)
    ppermute x12, waiting for transfers between devices, z_hop(): return lax.ppermute(block, 'seq', route)  51.3 us
    ppermute x7, waiting for transfers between devices, crossed(): lax.ppermute(block, 'seq', [(low, low ^ offset) for low in range(count)])  46.5 us
    dot_general x8, matrix products, swiglu_term(): return jnp.dot(hidden, down_rows, preferred_element_type=jnp.float32)  38.4 us
    ppermute x12, starting transfers between devices, z_hop(): return lax.ppermute(block, 'seq', route)  29 us
    all_to_all x1, starting transfers between devices, local(): lax.all_to_all(outgoing_place, ('grp', 'seq'), split_axis=0, concat_axis=...  26.1 us
    all_to_all x1, waiting for transfers between devices, local(): lax.all_to_all(outgoing, ('grp', 'seq'), split_axis=0, concat_axis=0, til...  20.3 us
    dot_general x8, matrix products, swiglu_term(): lax.dot_general(normed_rows, gate_rows, dims, preferred_element_type=jnp....  14.5 us
    unnamed x69, local copies, waits for them, and re-layouts  11.1 us
  transfers between devices with their start and end apart: 24, of which 12 were waited for; matrix products, arithmetic and copies ran while one was open for 26% of the time, Pallas kernels for 0%

profile of v1, /device:TPU:0, one launch (start us, length us, event | category | flops | bytes accessed | tf_op | source)
XLA Modules:
  0.0 309.6 jit_solution(13778642816962490730)
XLA Ops:
  3.4 5.9 %collective-permute-start.6 = (bf16[256,1536]{1,0:T(8,128)(2,1)S(1)}, bf16[256,1536]{1,0:T(8,128)(2,1)}, u32[]{:S(2)}, u32[]{:S(2)}) collective-permute-start(bf16[256,1536]{1,0:T(8,128)(2,1)S(1)} %fusion.20), channel_id=1, source_target_pairs={{0,2},{1,3},{2,4},{3,5},{4,6},{5,7},{8,10},{9,11},{10,12},{11,13},... | collective-permute-start | bytes 2359304 | tf_op jit(solution)/shard_map/ppermute | solution.py:26
  12.0 1.6 collective-permute-start.4
  17.5 12.8 %collective-permute-done.9 = bf16[256,1536]{1,0:T(8,128)(2,1)} collective-permute-done((bf16[256,1536]{1,0:T(8,128)(2,1)S(1)}, bf16[256,1536]{1,0:T(8,128)(2,1)}, u32[]{:S(2)}, u32[]{:S(2)}) %collective-permute-start.9) | collective-permute-done | bytes 786464 | tf_op jit(solution)/shard_map/ppermute | solution.py:26
  31.6 1.6 collective-permute-start.7
  33.2 16.3 %collective-permute-done = bf16[256,1536]{1,0:T(8,128)(2,1)} collective-permute-done((bf16[256,1536]{1,0:T(8,128)(2,1)}, bf16[256,1536]{1,0:T(8,128)(2,1)}, u32[]{:S(2)}, u32[]{:S(2)}) %collective-permute-start) | collective-permute-done | bytes 786464 | tf_op jit(solution)/shard_map/ppermute | solution.py:14
  50.7 14.2 %collective-permute-done.2 = bf16[256,1536]{1,0:T(8,128)(2,1)} collective-permute-done((bf16[256,1536]{1,0:T(8,128)(2,1)}, bf16[256,1536]{1,0:T(8,128)(2,1)}, u32[]{:S(2)}, u32[]{:S(2)}) %collective-permute-start.2) | collective-permute-done | bytes 786464 | tf_op jit(solution)/shard_map/ppermute | solution.py:14
  66.1 2.1 constant_dynamic-update-slice_fusion.3
  69.5 1.6 collective-permute-start.8
  72.3 1.8 broadcast_select_fusion.1
  78.3 4.3 %fusion.61 = f32[256,1536]{1,0:T(8,128)} fusion(bf16[512,1536]{1,0:T(8,128)(2,1)} %param.24, f32[256,512]{1,0:T(8,128)} %fusion.135, bf16[256,1536]{1,0:T(8,128)(2,1)S(1)} %broadcast_select_fusion.1, bf16[512,1536]{1,0:T(8,128)(2,1)} %param.23), kind=kOutput, calls=%fused_computation.89 | convolution fusion | flops 806092800 | bytes 6029312 | tf_op jit(solution)/shard_map/dot_general | solution.py:84
  82.6 7.7 %collective-permute-done.11 = bf16[256,1536]{1,0:T(8,128)(2,1)} collective-permute-done((bf16[256,1536]{1,0:T(8,128)(2,1)}, bf16[256,1536]{1,0:T(8,128)(2,1)}, u32[]{:S(2)}, u32[]{:S(2)}) %collective-permute-start.11) | collective-permute-done | bytes 786464 | tf_op jit(solution)/shard_map/ppermute | solution.py:26
  94.9 4.6 %fusion.62 = f32[256,1536]{1,0:T(8,128)} fusion(bf16[512,1536]{1,0:T(8,128)(2,1)} %param.24, f32[256,512]{1,0:T(8,128)} %fusion.137, bf16[256,1536]{1,0:T(8,128)(2,1)} %copy-done.11, bf16[512,1536]{1,0:T(8,128)(2,1)} %param.23), kind=kOutput, calls=%fused_computation.90 | convolution fusion | flops 806092800 | bytes 6029312 | tf_op jit(solution)/shard_map/dot_general | solution.py:84
  99.5 5.3 %fusion.115 = (bf16[256,1536]{1,0:T(8,128)(2,1)}, f32[256,1536]{1,0:T(8,128)}) fusion(f32[256,1536]{1,0:T(8,128)} %fusion.62, bf16[512,1536]{1,0:T(8,128)(2,1)} %copy-done.12, f32[256,512]{1,0:T(8,128)} %fusion.138, bf16[256,1536]{1,0:T(8,128)(2,1)} %copy-done.11, bf16[512,1536]{1,0:T(8,128)(2,1)} %constant_dynamic-update-slice_fusion.2), kind=kOutput, calls=%fused_computation.191 | convolution fusion | flops 806879232 | bytes 8388608 | tf_op jit(solution)/shard_map/dot_general | solution.py:84
  104.9 2.4 collective-permute-start.12
  107.2 4.8 %convolution_add_fusion.1 = f32[256,1536]{1,0:T(8,128)} fusion(f32[256,1536]{1,0:T(8,128)} %fusion.61, bf16[512,1536]{1,0:T(8,128)(2,1)} %copy-done.12, f32[256,512]{1,0:T(8,128)} %fusion.136, bf16[256,1536]{1,0:T(8,128)(2,1)S(1)} %broadcast_select_fusion.1, bf16[512,1536]{1,0:T(8,128)(2,1)} %constant_dynamic-update-slice_fusion.2), kind=kOutput, calls=%fused_computation.15 | convolution fusion | flops 806486016 | bytes 7602176 | tf_op jit(solution)/shard_map/dot_general | solution.py:84
  113.4 10.0 %collective-permute-done.12 = bf16[256,1536]{1,0:T(8,128)(2,1)} collective-permute-done((bf16[256,1536]{1,0:T(8,128)(2,1)}, bf16[256,1536]{1,0:T(8,128)(2,1)}, u32[]{:S(2)}, u32[]{:S(2)}) %collective-permute-start.12) | collective-permute-done | bytes 786464 | tf_op jit(solution)/shard_map/ppermute | solution.py:26
  123.4 2.3 add_convert_fusion.4
  125.7 5.4 %collective-permute-start.13 = (bf16[256,1536]{1,0:T(8,128)(2,1)}, bf16[256,1536]{1,0:T(8,128)(2,1)}, u32[]{:S(2)}, u32[]{:S(2)}) collective-permute-start(bf16[256,1536]{1,0:T(8,128)(2,1)} %add_convert_fusion.4), channel_id=1, source_target_pairs={{0,2},{1,3},{2,4},{3,5},{8,10},{9,11},{10,12},{11,13},{16,18},{17,... | collective-permute-start | bytes 2359304 | tf_op jit(solution)/shard_map/ppermute | solution.py:26
  133.9 4.3 %fusion.60 = f32[256,1536]{1,0:T(8,128)} fusion(bf16[512,1536]{1,0:T(8,128)(2,1)} %param.24, f32[256,512]{1,0:T(8,128)} %fusion.133, bf16[256,1536]{1,0:T(8,128)(2,1)S(1)} %broadcast_select_fusion.2, bf16[512,1536]{1,0:T(8,128)(2,1)} %param.23), kind=kOutput, calls=%fused_computation.88 | convolution fusion | flops 806092800 | bytes 6029312 | tf_op jit(solution)/shard_map/dot_general | solution.py:84
  138.2 8.2 %collective-permute-done.13 = bf16[256,1536]{1,0:T(8,128)(2,1)} collective-permute-done((bf16[256,1536]{1,0:T(8,128)(2,1)}, bf16[256,1536]{1,0:T(8,128)(2,1)}, u32[]{:S(2)}, u32[]{:S(2)}) %collective-permute-start.13) | collective-permute-done | bytes 786464 | tf_op jit(solution)/shard_map/ppermute | solution.py:26
  146.4 5.1 %add_convert_fusion.3 = (bf16[256,1536]{1,0:T(8,128)(2,1)}, bf16[256,1536]{1,0:T(8,128)(2,1)}) fusion(bf16[256,1536]{1,0:T(8,128)(2,1)} %collective-permute-done.13, f32[256,1536]{1,0:T(8,128)} %fusion.60, bf16[512,1536]{1,0:T(8,128)(2,1)} %copy-done.12, f32[256,512]{1,0:T(8,128)} %fusion.134, bf16[256,1536]{1,0:T(8,128)(2,1)S(1)} %broadcast_select_fusion.2, ...), kind=kOutput, calls=%fused_computation.39 | convolution fusion | flops 808058880 | bytes 8388608 | tf_op jit(solution)/shard_map/dot_general | solution.py:84
  152.4 2.6 add_convert_fusion.2
  155.0 1.6 collective-permute-start.16
  157.4 26.1 %all-to-all-start = ((s32[32,1,16]{2,1,0:T(1,128)}), s32[32,1,16]{2,1,0:T(1,128)S(1)}, u32[]{:S(2)}, u32[]{:S(2)}) async-start(s32[32,1,16]{2,1,0:T(1,128)} %bitcast), calls=%async_computation | async-start | bytes 32768 | tf_op jit(solution)/shard_map/all_to_all | solution.py:171
  183.7 2.9 fusion.131
  186.6 4.6 %collective-permute-start.14 = (bf16[256,1536]{1,0:T(8,128)(2,1)}, bf16[256,1536]{1,0:T(8,128)(2,1)}, u32[]{:S(2)}, u32[]{:S(2)}) collective-permute-start(bf16[256,1536]{1,0:T(8,128)(2,1)} %get-tuple-element.14), channel_id=1, source_target_pairs={{0,2},{1,3},{2,4},{3,5},{4,6},{5,7},{8,10},{9,11},{10,12},{11,13},... | collective-permute-start | bytes 2359304 | tf_op jit(solution)/shard_map/ppermute | solution.py:26
  191.2 2.4 add_convert_fusion.1
  195.0 4.3 %fusion.28 = f32[256,1536]{1,0:T(8,128)} fusion(bf16[512,1536]{1,0:T(8,128)(2,1)} %param.24, bf16[256,1536]{1,0:T(8,128)(2,1)S(1)} %copy-done.16, bf16[512,1536]{1,0:T(8,128)(2,1)} %param.23, f32[256,512]{1,0:T(8,128)} %fusion.131), kind=kOutput, calls=%fused_computation.52 | convolution fusion | flops 806092800 | bytes 6029312 | tf_op jit(solution)/shard_map/dot_general | solution.py:84
  199.3 3.2 %fusion.132 = f32[256,512]{1,0:T(8,128)} fusion(bf16[256,1536]{1,0:T(8,128)(2,1)} %copy-done.15, bf16[512,1536]{1,0:T(8,128)(2,1)} %copy-done.7), kind=kOutput, calls=%fused_computation.201 | convolution fusion | flops 402653184 | bytes 2883584 | tf_op jit(solution)/shard_map/dot_general | solution.py:81
  202.5 5.2 %collective-permute-done.14 = bf16[256,1536]{1,0:T(8,128)(2,1)} collective-permute-done((bf16[256,1536]{1,0:T(8,128)(2,1)}, bf16[256,1536]{1,0:T(8,128)(2,1)}, u32[]{:S(2)}, u32[]{:S(2)}) %collective-permute-start.14) | collective-permute-done | bytes 786464 | tf_op jit(solution)/shard_map/ppermute | solution.py:26
  207.7 7.4 %collective-permute-done.17 = bf16[256,1536]{1,0:T(8,128)(2,1)} collective-permute-done((bf16[256,1536]{1,0:T(8,128)(2,1)}, bf16[256,1536]{1,0:T(8,128)(2,1)}, u32[]{:S(2)}, u32[]{:S(2)}) %collective-permute-start.17) | collective-permute-done | bytes 786464 | tf_op jit(solution)/shard_map/ppermute | solution.py:26
  215.1 5.6 %fusion.116 = (f32[256]{0:T(256)S(1)}, f32[256,1536]{1,0:T(8,128)}) fusion(bf16[256,1536]{1,0:T(8,128)(2,1)} %collective-permute-done.17, bf16[256,1536]{1,0:T(8,128)(2,1)} %collective-permute-done.14, f32[256,1536]{1,0:T(8,128)} %fusion.28, bf16[512,1536]{1,0:T(8,128)(2,1)} %copy-done.12, f32[256,512]{1,0:T(8,128)} %fusion.132, f32[1536]{0:T(1024)S(1)} %copy-done.28, ...), kind=kOutput, calls=%fused_computation.192 | convolution fusion | flops 809631488 | bytes 9968640 | tf_op jit(solution)/shard_map/dot_general | solution.py:84
  220.7 1.7 multiply_reduce_fusion
  222.5 3.6 %convolution_convert_fusion.2 = bf16[512,768]{1,0:T(8,128)(2,1)} fusion(bf16[1536,768]{1,0:T(8,128)(2,1)S(1)} %copy-done, f32[256,1536]{1,0:T(8,128)} %get-tuple-element.23, f32[1536]{0:T(1024)S(1)} %copy-done.29, f32[1536]{0:T(1024)S(1)} %copy-done.30, f32[256]{0:T(256)S(1)} %add_rsqrt_fusion.1, f32[256]{0:T(256)S(1)} %broadcast_multiply_fusion.1, ...), kind=kOutput, calls=%fused_computation.41 | convolution fusion | flops 808189952 | bytes 4737024 | tf_op jit(solution)/shard_map/dot_general | solution.py:165
  226.1 3.7 %all-to-all-start.1 = ((bf16[32,16,768]{2,1,0:T(8,128)(2,1)}), bf16[32,16,768]{2,1,0:T(8,128)(2,1)S(1)}, u32[]{:S(2)}, u32[]{:S(2)}) async-start(bf16[32,16,768]{2,1,0:T(8,128)(2,1)} %bitcast.1), calls=%async_computation.1 | async-start | bytes 1572864 | tf_op jit(solution)/shard_map/all_to_all | solution.py:170
  231.5 20.3 %all-to-all-done.1 = bf16[32,16,768]{2,1,0:T(8,128)(2,1)S(1)} async-done(((bf16[32,16,768]{2,1,0:T(8,128)(2,1)}), bf16[32,16,768]{2,1,0:T(8,128)(2,1)S(1)}, u32[]{:S(2)}, u32[]{:S(2)}) %all-to-all-start.1) | async-done | bytes 786464 | tf_op jit(solution)/shard_map/all_to_all | solution.py:170
  252.3 2.2 collective-permute-start.19
  256.3 8.9 %collective-permute-done.20 = bf16[256,768]{1,0:T(8,128)(2,1)S(1)} collective-permute-done((bf16[256,768]{1,0:T(8,128)(2,1)S(1)}, bf16[256,768]{1,0:T(8,128)(2,1)S(1)}, u32[]{:S(2)}, u32[]{:S(2)}) %collective-permute-start.20) | collective-permute-done | bytes 393248 | tf_op jit(solution)/shard_map/ppermute | solution.py:14
  265.2 6.8 %collective-permute-done.19 = bf16[256,768]{1,0:T(8,128)(2,1)S(1)} collective-permute-done((bf16[256,768]{1,0:T(8,128)(2,1)S(1)}, bf16[256,768]{1,0:T(8,128)(2,1)S(1)}, u32[]{:S(2)}, u32[]{:S(2)}) %collective-permute-start.19) | collective-permute-done | bytes 393248 | tf_op jit(solution)/shard_map/ppermute | solution.py:14
  273.2 2.2 fusion.10
  275.4 2.6 convolution_convert_fusion
  278.7 4.6 %select_reduce_fusion.2 = (bf16[64,768]{1,0:T(8,128)(2,1)S(1)}, bf16[64,768]{1,0:T(8,128)(2,1)S(1)}, bf16[1024,768]{1,0:T(8,128)(2,1)}) fusion(pred[16,768]{1,0:T(8,128)(4,1)S(1)} %iota_compare_fusion.5, bf16[1024,768]{1,0:T(8,128)(2,1)} %convolution_convert_fusion, bf16[1024,768]{1,0:T(8,128)(2,1)S(1)} %fusion.10, bf16[768,768]{1,0:T(8,128)(2,1)} %param.35), kind=kOutput, calls=%fused_computation.34 | convolution fusion | flops 1211793408 | bytes 6107136 | tf_op jit(solution)/shard_map/dot_general | solution.py:192
  283.3 1.7 copy.41
  285.1 2.3 select_reduce_fusion
  287.4 4.5 %copy-done.2 = f32[12,256,1024]{2,1,0:T(8,128)} copy-done((f32[12,256,1024]{2,1,0:T(8,128)}, f32[12,256,1024]{2,1,0:T(8,128)S(1)}, u32[]{:S(2)}) %copy-start.2) | copy-done | bytes 12582936
  291.9 3.9 %fusion.1 = f32[12,256]{1,0:T(8,128)S(1)} fusion(f32[12,256,1024]{2,1,0:T(8,128)S(1)} %get-tuple-element.26, f32[12,256]{1,0:T(8,128)S(1)} %get-tuple-element.25, pred[256,1024]{1,0:T(8,128)(4,1)S(1)} %broadcast_compare_fusion), kind=kLoop, calls=%fused_computation.3 | loop fusion | flops 12579840 | bytes 12869632 | tf_op jit(solution)/shard_map/reduce_sum | solution.py:217
  295.8 1.6 copy.45
  301.4 6.9 %fusion.42 = bf16[256,12,64]{0,2,1:T(8,128)(2,1)S(1)} fusion(bf16[1024,12,64]{0,2,1:T(8,128)(2,1)} %bitcast.116, f32[12,256,1024]{2,1,0:T(8,128)} %copy-done.2, f32[12,256]{1,0:T(8,128)S(1)} %get-tuple-element.25, pred[256,1024]{1,0:T(8,128)(4,1)S(1)} %broadcast_compare_fusion, f32[256,12,64]{0,2,1:T(8,128)} %copy.47, f32[256,12]{0,1:T(8,128)S(1)} %get-tuple-element.11, ...), kind=kOutput, calls=%fused_computation.60 | convolution fusion | flops 416415744 | bytes 15659008 | tf_op jit(solution)/shard_map/hqk,khd->hqd/dot_general | solution.py:219
  (167 shorter events, 43.3 us)
Async XLA Ops:
  0.0 222.5 %copy-start = (bf16[1536,768]{1,0:T(8,128)(2,1)S(1)}, bf16[1536,768]{1,0:T(8,128)(2,1)}, u32[]{:S(2)}) copy-start(bf16[1536,768]{1,0:T(8,128)(2,1)} %param.28) | copy-start | bytes 7077892
  0.0 3.0 copy-start.13
  0.0 3.0 copy-start.22
  0.0 3.0 copy-start.23
  3.4 11.2 %copy-start.15 = (bf16[256,1536]{1,0:T(8,128)(2,1)}, bf16[256,1536]{1,0:T(8,128)(2,1)S(1)}, u32[]{:S(2)}) copy-start(bf16[256,1536]{1,0:T(8,128)(2,1)S(1)} %fusion.20) | copy-start | bytes 2359300
  3.4 28.2 %collective-permute-start.6 = (bf16[256,1536]{1,0:T(8,128)(2,1)S(1)}, bf16[256,1536]{1,0:T(8,128)(2,1)}, u32[]{:S(2)}, u32[]{:S(2)}) collective-permute-start(bf16[256,1536]{1,0:T(8,128)(2,1)S(1)} %fusion.20), channel_id=1, source_target_pairs={{0,2},{1,3},{2,4},{3,5},{4,6},{5,7},{8,10},{9,11},{10,12},{11,13},... | collective-permute-start | bytes 2359304 | tf_op jit(solution)/shard_map/ppermute | solution.py:26
  9.3 21.0 %collective-permute-start.9 = (bf16[256,1536]{1,0:T(8,128)(2,1)S(1)}, bf16[256,1536]{1,0:T(8,128)(2,1)}, u32[]{:S(2)}, u32[]{:S(2)}) collective-permute-start(bf16[256,1536]{1,0:T(8,128)(2,1)S(1)} %fusion.20), channel_id=1, source_target_pairs={{2,0},{3,1},{4,2},{5,3},{6,4},{7,5},{10,8},{11,9},{12,10},{13,11},... | collective-permute-start | bytes 2359304 | tf_op jit(solution)/shard_map/ppermute | solution.py:26
  10.6 3.0 copy-start.3
  10.7 4.4 %copy-start.21 = (bf16[512,1536]{1,0:T(8,128)(2,1)S(1)}, bf16[512,1536]{1,0:T(8,128)(2,1)}, u32[]{:S(2)}) copy-start(bf16[512,1536]{1,0:T(8,128)(2,1)} %param.23) | copy-start | bytes 4718596
  12.0 21.2 %collective-permute-start.4 = (bf16[256,1536]{1,0:T(8,128)(2,1)S(1)}, bf16[256,1536]{1,0:T(8,128)(2,1)}, u32[]{:S(2)}, u32[]{:S(2)}) collective-permute-start(bf16[256,1536]{1,0:T(8,128)(2,1)S(1)} %constant_dynamic-slice_fusion), channel_id=1, source_target_pairs={{0,1},{1,0},{2,3},{3,2},{4,5},{5,4},{6,7},{7,6},{8,9},{9,8},{10,11... | collective-permute-start | bytes 2359304 | tf_op jit(solution)/shard_map/ppermute | solution.py:14
  14.5 35.0 %collective-permute-start = (bf16[256,1536]{1,0:T(8,128)(2,1)}, bf16[256,1536]{1,0:T(8,128)(2,1)}, u32[]{:S(2)}, u32[]{:S(2)}) collective-permute-start(bf16[256,1536]{1,0:T(8,128)(2,1)} %constant_dynamic-slice_fusion.2), channel_id=1, source_target_pairs={{0,1},{1,0},{2,3},{3,2},{4,5},{5,4},{6,7},{7,6},{8,9},{9,8},{10,11... | collective-permute-start | bytes 2359304 | tf_op jit(solution)/shard_map/ppermute | solution.py:14
  16.0 48.9 %collective-permute-start.2 = (bf16[256,1536]{1,0:T(8,128)(2,1)}, bf16[256,1536]{1,0:T(8,128)(2,1)}, u32[]{:S(2)}, u32[]{:S(2)}) collective-permute-start(bf16[256,1536]{1,0:T(8,128)(2,1)} %constant_dynamic-slice_fusion.1), channel_id=1, source_target_pairs={{0,1},{1,0},{2,3},{3,2},{4,5},{5,4},{6,7},{7,6},{8,9},{9,8},{10,11... | collective-permute-start | bytes 2359304 | tf_op jit(solution)/shard_map/ppermute | solution.py:14
  30.3 37.9 %collective-permute-start.10 = (bf16[256,1536]{1,0:T(8,128)(2,1)}, bf16[256,1536]{1,0:T(8,128)(2,1)}, u32[]{:S(2)}, u32[]{:S(2)}) collective-permute-start(bf16[256,1536]{1,0:T(8,128)(2,1)} %collective-permute-done.9), channel_id=1, source_target_pairs={{2,0},{3,1},{4,2},{5,3},{10,8},{11,9},{12,10},{13,11},{18,16},{19,... | collective-permute-start | bytes 2359304 | tf_op jit(solution)/shard_map/ppermute | solution.py:26
  31.6 37.8 %collective-permute-start.7 = (bf16[256,1536]{1,0:T(8,128)(2,1)}, bf16[256,1536]{1,0:T(8,128)(2,1)}, u32[]{:S(2)}, u32[]{:S(2)}) collective-permute-start(bf16[256,1536]{1,0:T(8,128)(2,1)} %collective-permute-done.6), channel_id=1, source_target_pairs={{2,4},{3,5},{4,6},{5,7},{10,12},{11,13},{12,14},{13,15},{18,20},{1... | collective-permute-start | bytes 2359304 | tf_op jit(solution)/shard_map/ppermute | solution.py:26
  33.2 37.9 %collective-permute-start.5 = (bf16[256,1536]{1,0:T(8,128)(2,1)}, bf16[256,1536]{1,0:T(8,128)(2,1)S(1)}, u32[]{:S(2)}, u32[]{:S(2)}) collective-permute-start(bf16[256,1536]{1,0:T(8,128)(2,1)} %collective-permute-done.4), channel_id=1, source_target_pairs={{0,8},{8,0},{16,24},{24,16},{1,9},{9,1},{17,25},{25,17},{2,10},{10... | collective-permute-start | bytes 2359304 | tf_op jit(solution)/shard_map/ppermute | solution.py:67
  49.5 21.6 %collective-permute-start.1 = (bf16[256,1536]{1,0:T(8,128)(2,1)}, bf16[256,1536]{1,0:T(8,128)(2,1)S(1)}, u32[]{:S(2)}, u32[]{:S(2)}) collective-permute-start(bf16[256,1536]{1,0:T(8,128)(2,1)} %collective-permute-done), channel_id=1, source_target_pairs={{0,8},{8,0},{16,24},{24,16},{1,9},{9,1},{17,25},{25,17},{2,10},{10... | collective-permute-start | bytes 2359304 | tf_op jit(solution)/shard_map/ppermute | solution.py:67
  64.9 11.0 %collective-permute-start.3 = (bf16[256,1536]{1,0:T(8,128)(2,1)}, bf16[256,1536]{1,0:T(8,128)(2,1)S(1)}, u32[]{:S(2)}, u32[]{:S(2)}) collective-permute-start(bf16[256,1536]{1,0:T(8,128)(2,1)} %collective-permute-done.2), channel_id=1, source_target_pairs={{0,8},{8,0},{16,24},{24,16},{1,9},{9,1},{17,25},{25,17},{2,10},{10... | collective-permute-start | bytes 2359304 | tf_op jit(solution)/shard_map/ppermute | solution.py:67
  68.2 22.2 %collective-permute-start.11 = (bf16[256,1536]{1,0:T(8,128)(2,1)}, bf16[256,1536]{1,0:T(8,128)(2,1)}, u32[]{:S(2)}, u32[]{:S(2)}) collective-permute-start(bf16[256,1536]{1,0:T(8,128)(2,1)} %collective-permute-done.10), channel_id=1, source_target_pairs={{2,0},{3,1},{10,8},{11,9},{18,16},{19,17},{26,24},{27,25}} | collective-permute-start | bytes 2359304 | tf_op jit(solution)/shard_map/ppermute | solution.py:26
  69.5 42.5 %collective-permute-start.8 = (bf16[256,1536]{1,0:T(8,128)(2,1)}, bf16[256,1536]{1,0:T(8,128)(2,1)}, u32[]{:S(2)}, u32[]{:S(2)}) collective-permute-start(bf16[256,1536]{1,0:T(8,128)(2,1)} %collective-permute-done.7), channel_id=1, source_target_pairs={{4,6},{5,7},{12,14},{13,15},{20,22},{21,23},{28,30},{29,31}} | collective-permute-start | bytes 2359304 | tf_op jit(solution)/shard_map/ppermute | solution.py:26
  72.3 4.6 %copy-start.7 = (bf16[512,1536]{1,0:T(8,128)(2,1)}, bf16[512,1536]{1,0:T(8,128)(2,1)S(1)}, u32[]{:S(2)}) copy-start(bf16[512,1536]{1,0:T(8,128)(2,1)S(1)} %constant_dynamic-update-slice_fusion) | copy-start | bytes 4718596
  82.6 9.0 %copy-start.5 = (bf16[512,1536]{1,0:T(8,128)(2,1)S(1)}, bf16[512,1536]{1,0:T(8,128)(2,1)}, u32[]{:S(2)}) copy-start(bf16[512,1536]{1,0:T(8,128)(2,1)} %param.22) | copy-start | bytes 4718596
  104.9 18.5 %collective-permute-start.12 = (bf16[256,1536]{1,0:T(8,128)(2,1)}, bf16[256,1536]{1,0:T(8,128)(2,1)}, u32[]{:S(2)}, u32[]{:S(2)}) collective-permute-start(bf16[256,1536]{1,0:T(8,128)(2,1)} %get-tuple-element.20), channel_id=1, source_target_pairs={{0,2},{1,3},{8,10},{9,11},{16,18},{17,19},{24,26},{25,27}} | collective-permute-start | bytes 2359304 | tf_op jit(solution)/shard_map/ppermute | solution.py:26
  112.0 11.4 %copy-start.10 = (f32[256,1536]{1,0:T(8,128)S(1)}, f32[256,1536]{1,0:T(8,128)}, u32[]{:S(2)}) copy-start(f32[256,1536]{1,0:T(8,128)} %convolution_add_fusion.1) | copy-start | bytes 4718596
  113.4 17.7 %copy-start.6 = (bf16[512,1536]{1,0:T(8,128)(2,1)S(1)}, bf16[512,1536]{1,0:T(8,128)(2,1)}, u32[]{:S(2)}) copy-start(bf16[512,1536]{1,0:T(8,128)(2,1)} %param.22) | copy-start | bytes 4718596
  125.7 6.8 %copy-start.9 = (bf16[512,1536]{1,0:T(8,128)(2,1)S(1)}, bf16[512,1536]{1,0:T(8,128)(2,1)}, u32[]{:S(2)}) copy-start(bf16[512,1536]{1,0:T(8,128)(2,1)} %copy-done.7) | copy-start | bytes 4718596
  125.7 20.7 %collective-permute-start.13 = (bf16[256,1536]{1,0:T(8,128)(2,1)}, bf16[256,1536]{1,0:T(8,128)(2,1)}, u32[]{:S(2)}, u32[]{:S(2)}) collective-permute-start(bf16[256,1536]{1,0:T(8,128)(2,1)} %add_convert_fusion.4), channel_id=1, source_target_pairs={{0,2},{1,3},{2,4},{3,5},{8,10},{9,11},{10,12},{11,13},{16,18},{17,... | collective-permute-start | bytes 2359304 | tf_op jit(solution)/shard_map/ppermute | solution.py:26
  138.2 14.0 %copy-start.26 = (s32[256]{0:T(256)S(1)}, s32[256]{0:T(256)}, u32[]{:S(2)}) copy-start(s32[256]{0:T(256)} %param.30) | copy-start | bytes 3076
  151.5 0.9 collective-permute-start.15
  152.4 31.1 %copy-start.32 = (s32[1,4]{1,0:T(1,128)S(1)}, s32[1,4]{1,0:T(1,128)}, u32[]{:S(2)}) copy-start(s32[1,4]{1,0:T(1,128)} %param.31) | copy-start | bytes 52
  152.4 31.3 %copy-start.16 = (bf16[256,1536]{1,0:T(8,128)(2,1)S(1)}, bf16[256,1536]{1,0:T(8,128)(2,1)}, u32[]{:S(2)}) copy-start(bf16[256,1536]{1,0:T(8,128)(2,1)} %copy-done.15) | copy-start | bytes 2359300
  155.0 36.2 %collective-permute-start.16 = (bf16[256,1536]{1,0:T(8,128)(2,1)}, bf16[256,1536]{1,0:T(8,128)(2,1)}, u32[]{:S(2)}, u32[]{:S(2)}) collective-permute-start(bf16[256,1536]{1,0:T(8,128)(2,1)} %add_convert_fusion.2), channel_id=1, source_target_pairs={{4,2},{5,3},{6,4},{7,5},{12,10},{13,11},{14,12},{15,13},{20,18},{2... | collective-permute-start | bytes 2359304 | tf_op jit(solution)/shard_map/ppermute | solution.py:26
  157.4 68.7 %all-to-all-start = ((s32[32,1,16]{2,1,0:T(1,128)}), s32[32,1,16]{2,1,0:T(1,128)S(1)}, u32[]{:S(2)}, u32[]{:S(2)}) async-start(s32[32,1,16]{2,1,0:T(1,128)} %bitcast), calls=%async_computation | async-start | bytes 32768 | tf_op jit(solution)/shard_map/all_to_all | solution.py:171
  183.7 7.5 %copy-start.17 = (f32[256,1536]{1,0:T(8,128)S(1)}, f32[256,1536]{1,0:T(8,128)}, u32[]{:S(2)}) copy-start(f32[256,1536]{1,0:T(8,128)} %get-tuple-element.21) | copy-start | bytes 4718596
  186.6 21.1 %collective-permute-start.14 = (bf16[256,1536]{1,0:T(8,128)(2,1)}, bf16[256,1536]{1,0:T(8,128)(2,1)}, u32[]{:S(2)}, u32[]{:S(2)}) collective-permute-start(bf16[256,1536]{1,0:T(8,128)(2,1)} %get-tuple-element.14), channel_id=1, source_target_pairs={{0,2},{1,3},{2,4},{3,5},{4,6},{5,7},{8,10},{9,11},{10,12},{11,13},... | collective-permute-start | bytes 2359304 | tf_op jit(solution)/shard_map/ppermute | solution.py:26
  193.5 21.5 %collective-permute-start.17 = (bf16[256,1536]{1,0:T(8,128)(2,1)}, bf16[256,1536]{1,0:T(8,128)(2,1)}, u32[]{:S(2)}, u32[]{:S(2)}) collective-permute-start(bf16[256,1536]{1,0:T(8,128)(2,1)} %add_convert_fusion.1), channel_id=1, source_target_pairs={{2,0},{3,1},{4,2},{5,3},{6,4},{7,5},{10,8},{11,9},{12,10},{13,11},... | collective-permute-start | bytes 2359304 | tf_op jit(solution)/shard_map/ppermute | solution.py:26
  199.3 15.7 %copy-start.14 = (bf16[256,1536]{1,0:T(8,128)(2,1)S(1)}, bf16[256,1536]{1,0:T(8,128)(2,1)}, u32[]{:S(2)}) copy-start(bf16[256,1536]{1,0:T(8,128)(2,1)} %param.19) | copy-start | bytes 2359300
  199.3 15.7 %copy-start.28 = (f32[1536]{0:T(1024)S(1)}, f32[1536]{0:T(1024)}, u32[]{:S(2)}) copy-start(f32[1536]{0:T(1024)} %param.25) | copy-start | bytes 18436
  226.1 25.7 %all-to-all-start.1 = ((bf16[32,16,768]{2,1,0:T(8,128)(2,1)}), bf16[32,16,768]{2,1,0:T(8,128)(2,1)S(1)}, u32[]{:S(2)}, u32[]{:S(2)}) async-start(bf16[32,16,768]{2,1,0:T(8,128)(2,1)} %bitcast.1), calls=%async_computation.1 | async-start | bytes 1572864 | tf_op jit(solution)/shard_map/all_to_all | solution.py:170
  252.2 13.0 %collective-permute-start.20 = (bf16[256,768]{1,0:T(8,128)(2,1)S(1)}, bf16[256,768]{1,0:T(8,128)(2,1)S(1)}, u32[]{:S(2)}, u32[]{:S(2)}) collective-permute-start(bf16[256,768]{1,0:T(8,128)(2,1)S(1)} %convolution_convert_fusion.4), channel_id=1, source_target_pairs={{0,3},{1,2},{2,1},{3,0},{4,7},{5,6},{6,5},{7,4},{8,11},{9,10},{10,... | collective-permute-start | bytes 1179656 | tf_op jit(solution)/shard_map/ppermute | solution.py:14
  252.3 19.8 %collective-permute-start.19 = (bf16[256,768]{1,0:T(8,128)(2,1)S(1)}, bf16[256,768]{1,0:T(8,128)(2,1)S(1)}, u32[]{:S(2)}, u32[]{:S(2)}) collective-permute-start(bf16[256,768]{1,0:T(8,128)(2,1)S(1)} %convolution_convert_fusion.4), channel_id=1, source_target_pairs={{0,2},{1,3},{2,0},{3,1},{4,6},{5,7},{6,4},{7,5},{8,10},{9,11},{10,... | collective-permute-start | bytes 1179656 | tf_op jit(solution)/shard_map/ppermute | solution.py:14
  254.4 17.8 %collective-permute-start.18 = (bf16[256,768]{1,0:T(8,128)(2,1)S(1)}, bf16[256,768]{1,0:T(8,128)(2,1)S(1)}, u32[]{:S(2)}, u32[]{:S(2)}) collective-permute-start(bf16[256,768]{1,0:T(8,128)(2,1)S(1)} %convolution_convert_fusion.4), channel_id=1, source_target_pairs={{0,1},{1,0},{2,3},{3,2},{4,5},{5,4},{6,7},{7,6},{8,9},{9,8},{10,11... | collective-permute-start | bytes 1179656 | tf_op jit(solution)/shard_map/ppermute | solution.py:14
  256.3 16.9 %copy-start.24 = (f32[768]{0:T(1024)S(1)}, f32[768]{0:T(1024)}, u32[]{:S(2)}) copy-start(f32[768]{0:T(1024)} %param.33) | copy-start | bytes 9220
  256.3 16.9 %copy-start.25 = (f32[768]{0:T(1024)S(1)}, f32[768]{0:T(1024)}, u32[]{:S(2)}) copy-start(f32[768]{0:T(1024)} %param.32) | copy-start | bytes 9220
  285.0 12.6 %collective-permute-start.21 = (bf16[64,1536]{1,0:T(8,128)(2,1)S(1)}, bf16[64,1536]{1,0:T(8,128)(2,1)}, u32[]{:S(2)}, u32[]{:S(2)}) collective-permute-start(bf16[64,1536]{1,0:T(8,128)(2,1)S(1)} %pad_maximum_fusion.2), channel_id=1, source_target_pairs={{0,4},{1,5},{2,6},{3,7},{4,0},{5,1},{6,2},{7,3},{8,12},{9,13},{10,... | collective-permute-start | bytes 589832 | tf_op jit(solution)/shard_map/ppermute | solution.py:14
  287.4 4.5 %copy-start.2 = (f32[12,256,1024]{2,1,0:T(8,128)}, f32[12,256,1024]{2,1,0:T(8,128)S(1)}, u32[]{:S(2)}) copy-start(f32[12,256,1024]{2,1,0:T(8,128)S(1)} %get-tuple-element.26) | copy-start | bytes 37748740
  291.9 3.9 %copy-start.18 = (bf16[1024,768]{1,0:T(8,128)(2,1)S(1)}, bf16[1024,768]{1,0:T(8,128)(2,1)}, u32[]{:S(2)}) copy-start(bf16[1024,768]{1,0:T(8,128)(2,1)} %convolution_convert_fusion) | copy-start | bytes 4718596
  301.4 6.9 %copy-start.19 = (bf16[768,768]{1,0:T(8,128)(2,1)S(1)}, bf16[768,768]{1,0:T(8,128)(2,1)}, u32[]{:S(2)}) copy-start(bf16[768,768]{1,0:T(8,128)(2,1)} %param.37) | copy-start | bytes 3538948
  301.4 8.2 %copy-start.1 = (bf16[1536,768]{1,0:T(8,128)(2,1)S(1)}, bf16[1536,768]{1,0:T(8,128)(2,1)}, u32[]{:S(2)}) copy-start(bf16[1536,768]{1,0:T(8,128)(2,1)} %param.28) | copy-start | bytes 7077892
  (9 other events, 16.8 us)

commit v2 on v1

--- a/solution.py
+++ b/solution.py
@@ -1,6 +1,10 @@
+import functools
+
 import jax
 import jax.numpy as jnp
 from jax import lax
+from jax.experimental import pallas as pl
+from jax.experimental.pallas import tpu as pltpu
 from jax.sharding import PartitionSpec as P
 
 HEADS = 12
@@ -14,59 +18,330 @@
     return lax.ppermute(block, "seq", [(low, low ^ offset) for low in range(count)])
 
 
-def z_shape():
-    count = lax.axis_size("seq")
-    depth = min(4, count)
-    return depth, count // depth
-
-
-def z_hop(block, step, senders):
-    _, across = z_shape()
-    route = [(z * across + y, (z + step) * across + y) for z in senders for y in range(across)]
-    return lax.ppermute(block, "seq", route)
-
-
-def z_slots(block, z_index):
-    depth, _ = z_shape()
-    right, left = block, block
-    rights, lefts = {}, {}
-    for k in range(1, depth):
-        right = z_hop(right, 1, range(k - 1, depth - 1))
-        left = z_hop(left, -1, range(1, depth - k + 1))
-        rights[k], lefts[k] = right, left
-    return [block] + [
-        jnp.where(z_index >= k, rights[k], lefts[depth - k]) for k in range(1, depth)
+DEPTH = 4
+SPOT = {1: 0, 3: 1, 2: 2, 0: 3}
+
+
+def ffn_kernel(
+    across,
+    normed_ref,
+    gate_ref,
+    up_ref,
+    down_ref,
+    out_ref,
+    tiles,
+    weights,
+    sums,
+    right_out,
+    left_out,
+    right_in,
+    left_in,
+    local_sem,
+    tile_send,
+    tile_recv,
+    y_send,
+    y_recv,
+    twin_send,
+    twin_recv,
+    right_send,
+    right_recv,
+    left_send,
+    left_recv,
+):
+    seq = lax.axis_index("seq")
+    grp = lax.axis_index("grp")
+    z = seq // across
+    y = seq % across
+    core = grp % 2
+    twin = grp + 1 - 2 * core
+    has_right = z < DEPTH - 1
+    has_left = z > 0
+    rows = out_ref.shape[0]
+    count = gate_ref.shape[0]
+    half = count // 2
+    own = (gate_ref, up_ref, down_ref)
+
+    def y_peer(r):
+        return {"seq": z * across + (y + r) % across}
+
+    barrier = pltpu.get_barrier_semaphore()
+
+    @pl.when(has_right)
+    def _():
+        pl.semaphore_signal(barrier, inc=1, device_id={"seq": seq + across})
+
+    @pl.when(has_left)
+    def _():
+        pl.semaphore_signal(barrier, inc=1, device_id={"seq": seq - across})
+
+    for r in range(1, across):
+        pl.semaphore_signal(barrier, inc=1, device_id=y_peer(r))
+    pl.semaphore_signal(barrier, inc=1, device_id={"grp": twin})
+
+    loads = [pltpu.make_async_copy(normed_ref, tiles.at[SPOT[0]], local_sem.at[3])]
+    loads += [
+        pltpu.make_async_copy(own[i], weights.at[0, i], local_sem.at[i]) for i in range(3)
     ]
-
-
-def z_reduce(parts):
-    depth, _ = z_shape()
-    right = left = None
-    for t in range(1, depth):
-        to_right, to_left = parts[t], parts[depth - t]
-        if right is not None:
-            to_right, to_left = to_right + right, to_left + left
-        right = z_hop(to_right.astype(jnp.bfloat16), 1, range(t)).astype(jnp.float32)
-        left = z_hop(to_left.astype(jnp.bfloat16), -1, range(depth - t, depth)).astype(
-            jnp.float32
-        )
-    return parts[0] if right is None else parts[0] + right + left
-
-
-def y_weights(weights):
-    _, across = z_shape()
-    half = weights[0].shape[0] // 2
-    first = lax.axis_index("grp") % 2 * half
-    twins = [(low, low ^ 1) for low in range(lax.axis_size("grp"))]
-    out = []
-    for weight in weights:
-        mine = lax.dynamic_slice_in_dim(weight, first, half, 0)
-        pieces = []
-        for offset in range(1, across):
-            piece = crossed(mine, offset)
-            pieces += [piece, lax.ppermute(piece, "grp", twins)]
-        out.append(jnp.concatenate(pieces, 0) if pieces else None)
-    return out
+    for load in loads:
+        load.start()
+    pl.semaphore_wait(
+        barrier,
+        across + has_right.astype(jnp.int32) + has_left.astype(jnp.int32),
+    )
+    loads[0].wait()
+
+    def hop_right(k):
+        return pltpu.make_async_remote_copy(
+            src_ref=tiles.at[SPOT[k - 1]],
+            dst_ref=tiles.at[SPOT[k]],
+            send_sem=tile_send.at[0, k - 1],
+            recv_sem=tile_recv.at[k - 1],
+            device_id={"seq": seq + across},
+        )
+
+    def hop_left(k):
+        return pltpu.make_async_remote_copy(
+            src_ref=tiles.at[SPOT[(DEPTH - k + 1) % DEPTH]],
+            dst_ref=tiles.at[SPOT[DEPTH - k]],
+            send_sem=tile_send.at[1, k - 1],
+            recv_sem=tile_recv.at[DEPTH - k - 1],
+            device_id={"seq": seq - across},
+        )
+
+    mine = pl.ds(pl.multiple_of(core * half, half), half)
+    theirs = pl.ds(pl.multiple_of((1 - core) * half, half), half)
+
+    def y_copy(r, i):
+        return pltpu.make_async_remote_copy(
+            src_ref=own[i].at[mine],
+            dst_ref=weights.at[r, i, mine],
+            send_sem=y_send.at[r, i],
+            recv_sem=y_recv.at[r, i],
+            device_id=y_peer(r),
+        )
+
+    def twin_copy(r, i, part):
+        return pltpu.make_async_remote_copy(
+            src_ref=weights.at[r, i, part],
+            dst_ref=weights.at[r, i, part],
+            send_sem=twin_send.at[r, i],
+            recv_sem=twin_recv.at[r, i],
+            device_id={"grp": twin},
+        )
+
+    @pl.when(has_right)
+    def _():
+        hop_right(1).start()
+
+    @pl.when(has_left)
+    def _():
+        hop_left(1).start()
+
+    fetches = [(r, i) for r in range(1, across) for i in range(3)]
+    for r, i in fetches:
+        y_copy(r, i).start()
+
+    def relay(r, i):
+        y_copy(r, i).wait_recv()
+        twin_copy(r, i, mine).start()
+
+    marks = [len(fetches) // 3, 2 * len(fetches) // 3]
+    done = 0
+    for k in range(1, DEPTH):
+
+        @pl.when(z >= k)
+        def _():
+            hop_right(k).wait_recv()
+
+        if k < DEPTH - 1:
+
+            @pl.when((z >= k) & has_right)
+            def _():
+                hop_right(k + 1).start()
+
+        @pl.when(z <= DEPTH - 1 - k)
+        def _():
+            hop_left(k).wait_recv()
+
+        if k < DEPTH - 1:
+
+            @pl.when((z <= DEPTH - 1 - k) & has_left)
+            def _():
+                hop_left(k + 1).start()
+
+            while done < marks[k - 1]:
+                relay(*fetches[done])
+                done += 1
+    while done < len(fetches):
+        relay(*fetches[done])
+        done += 1
+    for load in loads[1:]:
+        load.wait()
+    for r, i in fetches:
+        twin_copy(r, i, theirs).wait_recv()
+
+    def products(first):
+        def step(index, carry):
+            spot = first + index // across
+            r = index % across
+            tile = tiles[spot]
+            dims = (((1,), (1,)), ((), ()))
+            gate = lax.dot_general(
+                tile, weights[r, 0], dims, preferred_element_type=jnp.float32
+            )
+            up_part = lax.dot_general(
+                tile, weights[r, 1], dims, preferred_element_type=jnp.float32
+            )
+            hidden = (gate / (1.0 + jnp.exp(-gate)) * up_part).astype(jnp.bfloat16)
+            term = jnp.dot(hidden, weights[r, 2], preferred_element_type=jnp.float32)
+
+            @pl.when(r == 0)
+            def _():
+                sums[spot] = term
+
+            @pl.when(r > 0)
+            def _():
+                sums[spot] += term
+
+            return carry
+
+        lax.fori_loop(0, 2 * across, step, 0)
+
+    def sum_right(t):
+        return pltpu.make_async_remote_copy(
+            src_ref=right_out.at[t - 1],
+            dst_ref=right_in.at[t - 1],
+            send_sem=right_send.at[t - 1],
+            recv_sem=right_recv.at[t - 1],
+            device_id={"seq": seq + across},
+        )
+
+    def sum_left(t):
+        return pltpu.make_async_remote_copy(
+            src_ref=left_out.at[t - 1],
+            dst_ref=left_in.at[t - 1],
+            send_sem=left_send.at[t - 1],
+            recv_sem=left_recv.at[t - 1],
+            device_id={"seq": seq - across},
+        )
+
+    def pass_on(t):
+        right_term, left_term = sums.at[SPOT[t]], sums.at[SPOT[DEPTH - t]]
+
+        @pl.when(z == 0)
+        def _():
+            right_out[t - 1] = right_term[...].astype(jnp.bfloat16)
+
+        @pl.when(z == DEPTH - 1)
+        def _():
+            left_out[t - 1] = left_term[...].astype(jnp.bfloat16)
+
+        if t > 1:
+
+            @pl.when((z >= 1) & (z <= t - 1))
+            def _():
+                sum_right(t - 1).wait_recv()
+                right_out[t - 1] = (
+                    right_term[...] + right_in[t - 2].astype(jnp.float32)
+                ).astype(jnp.bfloat16)
+
+        @pl.when((z <= t - 1) & has_right)
+        def _():
+            sum_right(t).start()
+
+        if t > 1:
+
+            @pl.when((z <= DEPTH - 2) & (z >= DEPTH - t))
+            def _():
+                sum_left(t - 1).wait_recv()
+                left_out[t - 1] = (
+                    left_term[...] + left_in[t - 2].astype(jnp.float32)
+                ).astype(jnp.bfloat16)
+
+        @pl.when((z >= DEPTH - t) & has_left)
+        def _():
+            sum_left(t).start()
+
+    products(0)
+    pass_on(1)
+    products(2)
+    pass_on(2)
+    pass_on(3)
+
+    @pl.when(has_left)
+    def _():
+        sum_right(DEPTH - 1).wait_recv()
+        sums[SPOT[0]] += right_in[DEPTH - 2].astype(jnp.float32)
+
+    @pl.when(has_right)
+    def _():
+        sum_left(DEPTH - 1).wait_recv()
+        sums[SPOT[0]] += left_in[DEPTH - 2].astype(jnp.float32)
+
+    out_ref[...] = sums[SPOT[0]]
+
+    for k in range(1, DEPTH):
+
+        @pl.when((z >= k - 1) & has_right)
+        def _():
+            hop_right(k).wait_send()
+
+        @pl.when((z <= DEPTH - k) & has_left)
+        def _():
+            hop_left(k).wait_send()
+
+        @pl.when((z <= k - 1) & has_right)
+        def _():
+            sum_right(k).wait_send()
+
+        @pl.when((z >= DEPTH - k) & has_left)
+        def _():
+            sum_left(k).wait_send()
+
+    for r, i in fetches:
+        y_copy(r, i).wait_send()
+        twin_copy(r, i, mine).wait_send()
+
+
+def ffn_sums(normed, gate_weight, up_weight, down_weight):
+    across = lax.axis_size("seq") // DEPTH
+    rows, width = normed.shape
+    count = gate_weight.shape[0]
+    messages = pltpu.VMEM((DEPTH - 1, rows, width), jnp.bfloat16)
+    sem = pltpu.SemaphoreType.DMA
+    flops = 6 * DEPTH * rows * across * count * width
+    return pl.pallas_call(
+        functools.partial(ffn_kernel, across),
+        out_shape=jax.ShapeDtypeStruct((rows, width), jnp.float32),
+        in_specs=[pl.BlockSpec(memory_space=pl.ANY)] * 4,
+        out_specs=pl.BlockSpec(memory_space=pltpu.VMEM),
+        scratch_shapes=[
+            pltpu.VMEM((DEPTH, rows, width), jnp.bfloat16),
+            pltpu.VMEM((across, 3, count, width), jnp.bfloat16),
+            pltpu.VMEM((DEPTH, rows, width), jnp.float32),
+            messages,
+            messages,
+            messages,
+            messages,
+            sem((4,)),
+            sem((2, DEPTH - 1)),
+            sem((DEPTH - 1,)),
+            sem((across, 3)),
+            sem((across, 3)),
+            sem((across, 3)),
+            sem((across, 3)),
+            sem((DEPTH - 1,)),
+            sem((DEPTH - 1,)),
+            sem((DEPTH - 1,)),
+            sem((DEPTH - 1,)),
+        ],
+        compiler_params=pltpu.CompilerParams(
+            collective_id=0, has_side_effects=True, vmem_limit_bytes=48 << 20
+        ),
+        cost_estimate=pl.CostEstimate(
+            flops=flops, bytes_accessed=6 * count * width, transcendentals=0
+        ),
+    )(normed, gate_weight, up_weight, down_weight)
 
 
 def layer_norm(values, gain_vec, bias_vector):
@@ -74,14 +349,6 @@
     centred = values - average
     variance = jnp.mean(centred * centred, -1, keepdims=True)
     return centred * lax.rsqrt(variance + 1e-06) * gain_vec + bias_vector
-
-
-def swiglu_term(normed_rows, gate_rows, up_rows, down_rows):
-    dims = (((1,), (1,)), ((), ()))
-    gate = lax.dot_general(normed_rows, gate_rows, dims, preferred_element_type=jnp.float32)
-    up_part = lax.dot_general(normed_rows, up_rows, dims, preferred_element_type=jnp.float32)
-    hidden = (jax.nn.silu(gate) * up_part).astype(jnp.bfloat16)
-    return jnp.dot(hidden, down_rows, preferred_element_type=jnp.float32)
 
 
 def pick_dilated(array):
@@ -135,15 +402,7 @@
     residual = tile_cls.astype(jnp.float32)
     normed = layer_norm(residual, ln_gain, ln_bias).astype(jnp.bfloat16)
     seq_index = lax.axis_index("seq")
-    _, across = z_shape()
-    far_gate, far_up, far_down = y_weights((gate_weight, up_weight, down_weight))
-    terms = []
-    for rows in z_slots(normed, seq_index // across):
-        term = swiglu_term(rows, gate_weight, up_weight, down_weight)
-        if across > 1:
-            term = term + swiglu_term(rows, far_gate, far_up, far_down)
-        terms.append(term)
-    mlp_out = z_reduce(terms)
+    mlp_out = ffn_sums(normed, gate_weight, up_weight, down_weight)
     tile_out = residual + layer_scale * mlp_out
     final = layer_norm(tile_out, final_gain, final_bias).astype(jnp.bfloat16)
     embed = (jnp.dot(final, proj_weight, preferred_element_type=jnp.float32) + proj_bias).astype(
@@ -158,20 +417,20 @@
     bucket = target * capacity + jnp.sum(same.astype(jnp.int32), 1)
     places = jnp.arange(devices * capacity, dtype=jnp.int32)
     sends = places[:, None] == bucket[None, :]
-    outgoing_place = (
-        jnp.sum(jnp.where(sends, position[None, :] - tile_rows, 0), 1) + tile_rows
-    ).reshape(devices, capacity)
+    lane = jnp.arange(128, dtype=jnp.int32)[None, :]
+    code = jnp.where(lane == 0, position[:, None] // 16, position[:, None] % 16)
+    code = jnp.where(lane < 2, code, 0) + (lane == 2)
+    tagged = jnp.concatenate([embed, code.astype(jnp.bfloat16)], 1)
     outgoing = (
-        jnp.dot(sends.astype(jnp.bfloat16), embed, preferred_element_type=jnp.float32)
+        jnp.dot(sends.astype(jnp.bfloat16), tagged, preferred_element_type=jnp.float32)
         .astype(jnp.bfloat16)
-        .reshape(devices, capacity, width)
-    )
-    incoming, incoming_place = (
-        lax.all_to_all(outgoing, ("grp", "seq"), split_axis=0, concat_axis=0, tiled=True),
-        lax.all_to_all(outgoing_place, ("grp", "seq"), split_axis=0, concat_axis=0, tiled=True),
-    )
-    arrived = incoming.reshape(-1, width)
-    arrived_place = incoming_place.reshape(-1)
+        .reshape(devices, capacity, width + 128)
+    )
+    incoming = lax.all_to_all(outgoing, ("grp", "seq"), split_axis=0, concat_axis=0, tiled=True)
+    incoming = incoming.reshape(-1, width + 128)
+    arrived = incoming[:, :width]
+    tags = incoming[:, width : width + 3].astype(jnp.int32)
+    arrived_place = jnp.where(tags[:, 2] == 1, tags[:, 0] * 16 + tags[:, 1], tile_rows)
     lands = (order[:, None] == arrived_place[None, :]).astype(jnp.bfloat16)
     placed = jnp.dot(lands, arrived, preferred_element_type=jnp.float32).astype(jnp.bfloat16)
     start_pos = seq_index * tile_rows

time: 311 us -> 234 us (0.75)
  Pallas kernels: 0 us -> 123 us
  waiting for transfers between devices: 118 us -> 31.6 us
  starting transfers between devices: 66 us -> 6.36 us
  matrix products: 75.5 us -> 26.4 us
    pallas_call x0 -> x1, Pallas kernels: none -> 123 us  [ffn_sums(): pl.pallas_call(functools.partial(ffn_kernel, across), out_shape=jax.Shape...]
    dot_general x17 -> x2, matrix products: 56.5 us -> 2.36 us  [the longest x1 1.38 us: local(): jnp.dot(sends.astype(jnp.bfloat16), tagged, preferred_element_type=jnp.fl...]
    ppermute x15 -> x0, waiting for transfers between devices: 51.3 us -> none  [the longest x12 51.3 us: z_hop(): return lax.ppermute(block, 'seq', route)]
    ppermute x7 -> x4, waiting for transfers between devices: 46.5 us -> 9.04 us  [crossed(): lax.ppermute(block, 'seq', [(low, low ^ offset) for low in range(count)])]
    ppermute x15 -> x0, starting transfers between devices: 29 us -> none  [the longest x12 29 us: z_hop(): return lax.ppermute(block, 'seq', route)]
    all_to_all x1 -> x0, starting transfers between devices: 26.1 us -> none  [local(): lax.all_to_all(outgoing_place, ('grp', 'seq'), split_axis=0, concat_axis=...]
    convert_element_type x3, other arithmetic: 7.2 us -> 0.17 us  [the longest x1 0.14 us: local(): tagged = jnp.concatenate([embed, code.astype(jnp.bfloat16)], 1)]
    unnamed x69 -> x54, local copies, waits for them, and re-layouts: 11.1 us -> 5.94 us
  transfers between devices with their start and end apart: 24 -> 5, of which waited for: 12 -> 4; matrix products, arithmetic and copies ran while one was open for 26% -> 8% of each run, Pallas kernels for 0% -> 0%
where the time goes in v2:
time: 234 us; the launch traced here: 233 us
  Pallas kernels  123 us (53%)
  waiting for transfers between devices  31.6 us (14%)
  matrix products  26.4 us (11%)
  other arithmetic  23.6 us (10%)
  local copies, waits for them, and re-layouts  21.6 us (9%)
  starting transfers between devices  6.36 us (3%)
    pallas_call x1, Pallas kernels, ffn_sums(): pl.pallas_call(functools.partial(ffn_kernel, across), out_shape=jax.Shape...  123 us
    all_to_all x1, waiting for transfers between devices, local(): lax.all_to_all(outgoing, ('grp', 'seq'), split_axis=0, concat_axis=0, til...  22.6 us
    ppermute x4, waiting for transfers between devices, crossed(): lax.ppermute(block, 'seq', [(low, low ^ offset) for low in range(count)])  9.04 us
    dot_general x1, matrix products, local(): jnp.einsum('hqk,khd->hqd', weights.astype(jnp.bfloat16), all_values, pref...  6.82 us
    unnamed x54, local copies, waits for them, and re-layouts  5.94 us
    dot_general x1, matrix products, local(): jnp.dot(normed_seq, k_weight, preferred_element_type=jnp.float32)  5.65 us
  transfers between devices with their start and end apart: 5, of which 4 were waited for; matrix products, arithmetic and copies ran while one was open for 8% of the time, Pallas kernels for 0%

profile of v2, /device:TPU:0, one launch (start us, length us, event | category | flops | bytes accessed | tf_op | source)
XLA Modules:
  0.0 232.9 jit_solution(16183979071865335615)
XLA Ops:
  0.0 0.8 and_select_fusion.1
  1.1 1.5 convert_reduce_fusion.1
  2.6 1.5 fusion.13
  4.1 1.5 fusion.16.normed_ref
  5.6 122.8 %shard_map.181 = f32[256,1536]{1,0:T(8,128)S(1)} custom-call(bf16[256,1536]{1,0:T(8,128)(2,1)S(1)} %fusion.16.normed_ref, bf16[512,1536]{1,0:T(8,128)(2,1)S(1)} %copy-done.1, bf16[512,1536]{1,0:T(8,128)(2,1)S(1)} %copy-done.2, bf16[512,1536]{1,0:T(8,128)(2,1)} %down_ref.1), custom_call_target="tpu_custom_call" | custom-call | flops 9663676416 | bytes 4718592 | tf_op jit(solution)/shard_map/pallas_call | solution.py:313
  128.4 0.3 fusion.47
  128.7 0.4 multiply_reduce_fusion
  129.4 1.0 fusion.20
  130.4 1.4 convolution_convert_fusion.2
  131.8 2.8 %all-to-all-start = ((bf16[32,16,896]{2,1,0:T(8,128)(2,1)}), bf16[32,16,896]{2,1,0:T(8,128)(2,1)S(1)}, u32[]{:S(2)}, u32[]{:S(2)}) async-start(bf16[32,16,896]{2,1,0:T(8,128)(2,1)} %bitcast.77), calls=%async_computation | async-start | bytes 1835008 | tf_op jit(solution)/shard_map/all_to_all | solution.py:429
  135.1 0.3 copy-done.21
  135.4 0.6 iota_add_fusion
  136.0 0.6 slice_bitcast_fusion
  136.6 22.6 %all-to-all-done = bf16[32,16,896]{2,1,0:T(8,128)(2,1)S(1)} async-done(((bf16[32,16,896]{2,1,0:T(8,128)(2,1)}), bf16[32,16,896]{2,1,0:T(8,128)(2,1)S(1)}, u32[]{:S(2)}, u32[]{:S(2)}) %all-to-all-start) | async-done | bytes 917536 | tf_op jit(solution)/shard_map/all_to_all | solution.py:429
  159.2 0.9 copy-done.7
  160.1 0.3 fusion.50
  160.4 1.5 convolution_convert_fusion.4
  162.0 2.2 collective-permute-start.1
  164.2 1.3 collective-permute-start
  165.5 0.6 iota_compare_fusion.6
  166.1 1.4 copy.47
  167.5 1.3 tile.13
  168.8 1.4 tile.14
  170.2 1.4 convert_reduce_fusion.3
  171.6 1.5 broadcast_compare_fusion
  173.1 1.9 collective-permute-done.2
  175.0 6.8 %collective-permute-done.1 = bf16[256,768]{1,0:T(8,128)(2,1)S(1)} collective-permute-done((bf16[256,768]{1,0:T(8,128)(2,1)S(1)}, bf16[256,768]{1,0:T(8,128)(2,1)S(1)}, u32[]{:S(2)}, u32[]{:S(2)}) %collective-permute-start.1) | collective-permute-done | bytes 393248 | tf_op jit(solution)/shard_map/ppermute | solution.py:18
  181.8 0.4 collective-permute-done
  182.2 1.3 convert_reduce_fusion
  183.4 1.6 fusion.7
  185.1 3.0 %fusion.10 = bf16[1024,768]{1,0:T(8,128)(2,1)S(1)} fusion(f32[768]{0:T(1024)S(1)} %copy-done.19, f32[768]{0:T(1024)S(1)} %copy-done.20, f32[1024]{0:T(1024)S(1)} %add_rsqrt_fusion, f32[1024]{0:T(1024)S(1)} %broadcast_multiply_fusion, bf16[256,768]{1,0:T(8,128)(2,1)S(1)} %collective-permute-done.2, bf16[256,768]{1,0:T(8,128)(2,1)S(1)} %collective-permute-done.1, ...), kind=kLoop, calls=%fused_computation.13 | loop fusion | flops 10223616 | bytes 3160064 | tf_op jit(solution)/shard_map/convert_element_type | solution.py:447
  188.2 2.5 %convolution_convert_fusion = bf16[1024,768]{1,0:T(8,128)(2,1)} fusion(bf16[1024,768]{1,0:T(8,128)(2,1)S(1)} %fusion.10, bf16[768,768]{1,0:T(8,128)(2,1)S(1)} %copy-done.22), kind=kOutput, calls=%fused_computation.19 | convolution fusion | flops 1208745984 | bytes 4325376 | tf_op jit(solution)/shard_map/dot_general | solution.py:454
  190.7 1.1 select_reduce_fusion.3
  192.0 5.7 %select_reduce_fusion.2 = (bf16[64,768]{1,0:T(8,128)(2,1)S(1)}, bf16[64,768]{1,0:T(8,128)(2,1)}, bf16[1024,768]{1,0:T(8,128)(2,1)}) fusion(pred[16,768]{1,0:T(8,128)(4,1)S(1)} %iota_compare_fusion.5, bf16[1024,768]{1,0:T(8,128)(2,1)} %convolution_convert_fusion, bf16[1024,768]{1,0:T(8,128)(2,1)} %copy-done.5, bf16[768,768]{1,0:T(8,128)(2,1)} %param.35), kind=kOutput, calls=%fused_computation.27 | convolution fusion | flops 1211793408 | bytes 6107136 | tf_op jit(solution)/shard_map/dot_general | solution.py:451
  197.7 2.6 %copy.46 = bf16[1024,768]{0,1:T(8,128)(2,1)} copy(bf16[1024,768]{1,0:T(8,128)(2,1)} %get-tuple-element.19) | data formatting | bytes 3145728 | tf_op jit(solution)/shard_map/convert_element_type | solution.py:451
  200.3 1.6 pad_maximum_fusion.2
  201.9 3.7 %select_reduce_fusion = (f32[12,256]{1,0:T(8,128)S(1)}, f32[12,256,1024]{2,1,0:T(8,128)S(1)}) fusion(pred[256,1024]{1,0:T(8,128)(4,1)S(1)} %copy-done.6, bf16[256,12,64]{0,2,1:T(8,128)(2,1)S(1)} %bitcast.74, bf16[1024,12,64]{0,2,1:T(8,128)(2,1)} %bitcast.72), kind=kOutput, calls=%fused_computation.1 | convolution fusion | flops 412087296 | bytes 14823424 | tf_op jit(solution)/shard_map/qhd,khd->hqk/dot_general | solution.py:471
  205.6 4.6 %copy-done.3 = f32[12,256,1024]{2,1,0:T(8,128)} copy-done((f32[12,256,1024]{2,1,0:T(8,128)}, f32[12,256,1024]{2,1,0:T(8,128)S(1)}, u32[]{:S(2)}) %copy-start.3) | copy-done | bytes 12582936
  210.2 3.9 %fusion.1 = f32[12,256]{1,0:T(8,128)S(1)} fusion(f32[12,256,1024]{2,1,0:T(8,128)S(1)} %get-tuple-element.21, f32[12,256]{1,0:T(8,128)S(1)} %get-tuple-element.20, pred[256,1024]{1,0:T(8,128)(4,1)S(1)} %copy-done.6), kind=kLoop, calls=%fused_computation.3 | loop fusion | flops 12579840 | bytes 12869632 | tf_op jit(solution)/shard_map/reduce_sum | solution.py:476
  214.1 2.6 %copy.50 = bf16[1024,768]{0,1:T(8,128)(2,1)} copy(bf16[1024,768]{1,0:T(8,128)(2,1)} %convolution_convert_fusion) | data formatting | bytes 3145728 | tf_op jit(solution)/shard_map/convert_element_type | solution.py:454
  216.9 1.0 pad_maximum_fusion.1
  217.9 0.8 copy.51
  218.9 0.2 fusion.54
  219.3 1.2 fusion.23
  220.5 1.3 broadcast_in_dim.121
  221.8 2.8 %copy.52 = f32[256,12,64]{0,2,1:T(8,128)} copy(f32[256,12,64]{2,0,1:T(8,128)} %bitcast.71) | data formatting | bytes 1572864 | tf_op jit(solution)/shard_map/reshape | solution.py:366
  224.8 6.8 %fusion.36 = bf16[256,12,64]{0,2,1:T(8,128)(2,1)S(1)} fusion(bf16[1024,12,64]{0,2,1:T(8,128)(2,1)} %bitcast.73, f32[12,256,1024]{2,1,0:T(8,128)} %copy-done.3, f32[12,256]{1,0:T(8,128)S(1)} %get-tuple-element.20, pred[256,1024]{1,0:T(8,128)(4,1)S(1)} %copy-done.6, f32[256,12,64]{0,2,1:T(8,128)} %copy.52, f32[256,12]{0,1:T(8,128)S(1)} %get-tuple-element.11, ...), kind=kOutput, calls=%fused_computation.46 | convolution fusion | flops 416415744 | bytes 15659008 | tf_op jit(solution)/shard_map/hqk,khd->hqd/dot_general | solution.py:478
  231.7 1.3 fusion.22
  (88 shorter events, 2.0 us)
Async XLA Ops:
  0.0 129.3 %copy-start = (bf16[1536,768]{1,0:T(8,128)(2,1)S(1)}, bf16[1536,768]{1,0:T(8,128)(2,1)}, u32[]{:S(2)}) copy-start(bf16[1536,768]{1,0:T(8,128)(2,1)} %param.28) | copy-start | bytes 7077892
  0.0 4.0 %copy-start.17 = (f32[1536]{0:T(1024)S(1)}, f32[1536]{0:T(1024)}, u32[]{:S(2)}) copy-start(f32[1536]{0:T(1024)} %param.21) | copy-start | bytes 18436
  0.0 4.1 %copy-start.18 = (f32[1536]{0:T(1024)S(1)}, f32[1536]{0:T(1024)}, u32[]{:S(2)}) copy-start(f32[1536]{0:T(1024)} %param.20) | copy-start | bytes 18436
  1.1 4.5 %copy-start.1 = (bf16[512,1536]{1,0:T(8,128)(2,1)S(1)}, bf16[512,1536]{1,0:T(8,128)(2,1)}, u32[]{:S(2)}) copy-start(bf16[512,1536]{1,0:T(8,128)(2,1)} %gate_ref.1) | copy-start | bytes 4718596
  1.1 4.5 %copy-start.2 = (bf16[512,1536]{1,0:T(8,128)(2,1)S(1)}, bf16[512,1536]{1,0:T(8,128)(2,1)}, u32[]{:S(2)}) copy-start(bf16[512,1536]{1,0:T(8,128)(2,1)} %up_ref.1) | copy-start | bytes 4718596
  5.6 122.8 %copy-start.4 = (bf16[256,1536]{1,0:T(8,128)(2,1)S(1)}, bf16[256,1536]{1,0:T(8,128)(2,1)}, u32[]{:S(2)}) copy-start(bf16[256,1536]{1,0:T(8,128)(2,1)} %param.19) | copy-start | bytes 2359300
  5.6 122.8 %copy-start.14 = (f32[1536]{0:T(1024)S(1)}, f32[1536]{0:T(1024)}, u32[]{:S(2)}) copy-start(f32[1536]{0:T(1024)} %param.25) | copy-start | bytes 18436
  128.7 0.7 copy-start.23
  128.7 0.7 copy-start.24
  128.7 0.7 copy-start.25
  130.4 4.2 %copy-start.26 = (s32[1,4]{1,0:T(1,128)S(1)}, s32[1,4]{1,0:T(1,128)}, u32[]{:S(2)}) copy-start(s32[1,4]{1,0:T(1,128)} %param.31) | copy-start | bytes 52
  131.8 27.4 %all-to-all-start = ((bf16[32,16,896]{2,1,0:T(8,128)(2,1)}), bf16[32,16,896]{2,1,0:T(8,128)(2,1)S(1)}, u32[]{:S(2)}, u32[]{:S(2)}) async-start(bf16[32,16,896]{2,1,0:T(8,128)(2,1)} %bitcast.77), calls=%async_computation | async-start | bytes 1835008 | tf_op jit(solution)/shard_map/all_to_all | solution.py:429
  134.8 0.5 copy-start.21
  134.9 27.0 %copy-start.15 = (s32[256]{0:T(256)}, s32[256]{0:T(256)S(1)}, u32[]{:S(2)}) copy-start(s32[256]{0:T(256)S(1)} %get-tuple-element.7) | copy-start | bytes 3076
  159.2 0.9 copy-start.7
  162.0 13.0 %collective-permute-start.2 = (bf16[256,768]{1,0:T(8,128)(2,1)S(1)}, bf16[256,768]{1,0:T(8,128)(2,1)S(1)}, u32[]{:S(2)}, u32[]{:S(2)}) collective-permute-start(bf16[256,768]{1,0:T(8,128)(2,1)S(1)} %convolution_convert_fusion.4), channel_id=1, source_target_pairs={{0,3},{1,2},{2,1},{3,0},{4,7},{5,6},{6,5},{7,4},{8,11},{9,10},{10,... | collective-permute-start | bytes 1179656 | tf_op jit(solution)/shard_map/ppermute | solution.py:18
  162.0 19.7 %collective-permute-start.1 = (bf16[256,768]{1,0:T(8,128)(2,1)S(1)}, bf16[256,768]{1,0:T(8,128)(2,1)S(1)}, u32[]{:S(2)}, u32[]{:S(2)}) collective-permute-start(bf16[256,768]{1,0:T(8,128)(2,1)S(1)} %convolution_convert_fusion.4), channel_id=1, source_target_pairs={{0,2},{1,3},{2,0},{3,1},{4,6},{5,7},{6,4},{7,5},{8,10},{9,11},{10,... | collective-permute-start | bytes 1179656 | tf_op jit(solution)/shard_map/ppermute | solution.py:18
  164.2 18.0 %collective-permute-start = (bf16[256,768]{1,0:T(8,128)(2,1)S(1)}, bf16[256,768]{1,0:T(8,128)(2,1)}, u32[]{:S(2)}, u32[]{:S(2)}) collective-permute-start(bf16[256,768]{1,0:T(8,128)(2,1)S(1)} %convolution_convert_fusion.4), channel_id=1, source_target_pairs={{0,1},{1,0},{2,3},{3,2},{4,5},{5,4},{6,7},{7,6},{8,9},{9,8},{10,11... | collective-permute-start | bytes 1179656 | tf_op jit(solution)/shard_map/ppermute | solution.py:18
  173.1 11.9 %copy-start.19 = (f32[768]{0:T(1024)S(1)}, f32[768]{0:T(1024)}, u32[]{:S(2)}) copy-start(f32[768]{0:T(1024)} %param.33) | copy-start | bytes 9220
  173.1 11.9 %copy-start.20 = (f32[768]{0:T(1024)S(1)}, f32[768]{0:T(1024)}, u32[]{:S(2)}) copy-start(f32[768]{0:T(1024)} %param.32) | copy-start | bytes 9220
  185.1 3.1 %copy-start.22 = (bf16[768,768]{1,0:T(8,128)(2,1)S(1)}, bf16[768,768]{1,0:T(8,128)(2,1)}, u32[]{:S(2)}) copy-start(bf16[768,768]{1,0:T(8,128)(2,1)} %param.36) | copy-start | bytes 3538948
  188.1 2.6 %copy-start.5 = (bf16[1024,768]{1,0:T(8,128)(2,1)}, bf16[1024,768]{1,0:T(8,128)(2,1)S(1)}, u32[]{:S(2)}) copy-start(bf16[1024,768]{1,0:T(8,128)(2,1)S(1)} %fusion.10) | copy-start | bytes 4718596
  188.1 2.6 %copy-start.9 = (bf16[768,768]{1,0:T(8,128)(2,1)S(1)}, bf16[768,768]{1,0:T(8,128)(2,1)}, u32[]{:S(2)}) copy-start(bf16[768,768]{1,0:T(8,128)(2,1)} %param.34) | copy-start | bytes 3538948
  197.7 4.2 %copy-start.6 = (pred[256,1024]{1,0:T(8,128)(4,1)S(1)}, pred[256,1024]{1,0:T(8,128)(4,1)}, u32[]{:S(2)}) copy-start(pred[256,1024]{1,0:T(8,128)(4,1)} %broadcast_compare_fusion) | copy-start | bytes 786436
  201.9 15.0 %collective-permute-start.3 = (bf16[64,1536]{1,0:T(8,128)(2,1)}, bf16[64,1536]{1,0:T(8,128)(2,1)}, u32[]{:S(2)}, u32[]{:S(2)}) collective-permute-start(bf16[64,1536]{1,0:T(8,128)(2,1)} %pad_maximum_fusion.2), channel_id=1, source_target_pairs={{0,4},{1,5},{2,6},{3,7},{4,0},{5,1},{6,2},{7,3},{8,12},{9,13},{10,... | collective-permute-start | bytes 589832 | tf_op jit(solution)/shard_map/ppermute | solution.py:18
  205.6 4.6 %copy-start.3 = (f32[12,256,1024]{2,1,0:T(8,128)}, f32[12,256,1024]{2,1,0:T(8,128)S(1)}, u32[]{:S(2)}) copy-start(f32[12,256,1024]{2,1,0:T(8,128)S(1)} %get-tuple-element.21) | copy-start | bytes 37748740
  214.1 2.7 %copy-start.11 = (bf16[16,768]{1,0:T(8,128)(2,1)S(1)}, bf16[16,768]{1,0:T(8,128)(2,1)}, u32[]{:S(2)}) copy-start(bf16[16,768]{1,0:T(8,128)(2,1)} %get-tuple-element.22) | copy-start | bytes 73732
  214.1 2.8 %copy-start.10 = (bf16[64,768]{1,0:T(8,128)(2,1)S(1)}, bf16[64,768]{1,0:T(8,128)(2,1)}, u32[]{:S(2)}) copy-start(bf16[64,768]{1,0:T(8,128)(2,1)} %get-tuple-element.6) | copy-start | bytes 294916
  216.7 2.1 copy-start.12
  216.7 2.1 copy-start.13
  221.8 3.0 %copy-start.16 = (pred[256,12]{0,1:T(8,128)(4,1)S(1)}, pred[256,12]{0,1:T(8,128)(4,1)}, u32[]{:S(2)}) copy-start(pred[256,12]{0,1:T(8,128)(4,1)} %tile.14) | copy-start | bytes 9220
  224.8 6.8 %copy-start.8 = (bf16[768,768]{1,0:T(8,128)(2,1)S(1)}, bf16[768,768]{1,0:T(8,128)(2,1)}, u32[]{:S(2)}) copy-start(bf16[768,768]{1,0:T(8,128)(2,1)} %param.37) | copy-start | bytes 3538948

commit v3 on v2

--- a/solution.py
+++ b/solution.py
@@ -358,22 +358,122 @@
     return jnp.sum(jnp.where(own[None], grid, 0), 1, dtype=jnp.float32).astype(array.dtype)
 
 
-def combine(local_out, local_lse, far_out, far_lse, length):
-    picked = length // RATE
-    chosen = jnp.tile(jnp.arange(RATE)[:, None] == jnp.arange(HEADS)[None, :], (picked, 1))
-    distant_output_total = jnp.broadcast_to(
-        jnp.transpose(far_out, (1, 0, 2))[:, None], (picked, RATE, HEADS, HEAD_DIM)
-    ).reshape(length, HEADS, HEAD_DIM)
-    distant_logsumexp_total = jnp.broadcast_to(
-        jnp.transpose(far_lse)[:, None], (picked, RATE, HEADS)
-    ).reshape(length, HEADS)
-    peak = jnp.where(chosen, jnp.maximum(local_lse, distant_logsumexp_total), local_lse)
-    local_share = jnp.exp(local_lse - peak)
-    far_share = jnp.where(chosen, jnp.exp(distant_logsumexp_total - peak), 0.0)
-    mixed = (local_share[..., None] * local_out + far_share[..., None] * distant_output_total) / (
-        local_share + far_share
-    )[..., None]
-    return mixed.reshape(length, HEADS * HEAD_DIM)
+def attention_kernel(
+    ends_ref,
+    query_pos_ref,
+    key_pos_ref,
+    far_pos_ref,
+    query_ref,
+    key_ref,
+    value_ref,
+    far_key_ref,
+    far_value_ref,
+    o_ref,
+    resid_ref,
+    out_ref,
+    total,
+):
+    pair = pl.program_id(0)
+
+    def slides(spots):
+        return sum((spots >= ends_ref[j]).astype(jnp.int32) for j in range(ends_ref.shape[0]))
+
+    @pl.when(pair == 0)
+    def _():
+        total[...] = resid_ref[...].astype(jnp.float32)
+
+    query_pos = query_pos_ref[...]
+    query_slide = slides(query_pos)
+    near = query_slide == slides(key_pos_ref[...])
+    query = query_ref[...] * HEAD_DIM ** (-0.5)
+    lane = lax.broadcasted_iota(jnp.int32, query.shape, 1)
+    dims = (((1,), (1,)), ((), ()))
+    results = []
+    for which in range(2):
+        head = 2 * pair + which
+        far = (query_slide == slides(far_pos_ref[...] + head)) & (query_pos % RATE == head)
+        masked = jnp.where(lane // HEAD_DIM == which, query, jnp.zeros_like(query))
+        scores = lax.dot_general(
+            masked, key_ref[...], dims, preferred_element_type=jnp.float32
+        )
+        far_scores = lax.dot_general(
+            masked, far_key_ref[...], dims, preferred_element_type=jnp.float32
+        )
+        scores = jnp.where(near, scores, -1e30)
+        far_scores = jnp.where(far, far_scores, -1e30)
+        peak = jnp.maximum(
+            jnp.max(scores, -1, keepdims=True), jnp.max(far_scores, -1, keepdims=True)
+        )
+        share = jnp.exp(scores - peak)
+        far_share = jnp.exp(far_scores - peak)
+        weight = jnp.sum(share, -1, keepdims=True) + jnp.sum(far_share, -1, keepdims=True)
+        mixed = jnp.dot(
+            share.astype(jnp.bfloat16), value_ref[...], preferred_element_type=jnp.float32
+        ) + jnp.dot(
+            far_share.astype(jnp.bfloat16),
+            far_value_ref[...],
+            preferred_element_type=jnp.float32,
+        )
+        results.append(mixed / weight)
+    attn = jnp.where(lane < HEAD_DIM, results[0], results[1]).astype(jnp.bfloat16)
+    total[...] += jnp.dot(attn, o_ref[...], preferred_element_type=jnp.float32)
+
+    @pl.when(pair == pl.num_programs(0) - 1)
+    def _():
+        out_ref[...] = total[...].astype(jnp.bfloat16)
+
+
+def attend(ends, query_pos, key_pos, far_pos, queries, keys, values, far_rows, o_weight, placed):
+    rows, width = placed.shape
+    pairs = width // 128
+    key_count, far_count = keys.shape[0], far_rows.shape[0]
+
+    def whole(array):
+        return pl.BlockSpec(array.shape, lambda j: (0, 0))
+
+    def column(count, first=0):
+        return pl.BlockSpec((count, 128), lambda j: (0, first + j))
+
+    return pl.pallas_call(
+        attention_kernel,
+        out_shape=jax.ShapeDtypeStruct((rows, width), jnp.bfloat16),
+        grid=(pairs,),
+        in_specs=[
+            pl.BlockSpec(memory_space=pltpu.SMEM),
+            whole(query_pos),
+            whole(key_pos),
+            whole(far_pos),
+            column(rows),
+            column(key_count),
+            column(key_count),
+            column(far_count),
+            column(far_count, pairs),
+            pl.BlockSpec((128, width), lambda j: (j, 0)),
+            whole(placed),
+        ],
+        out_specs=pl.BlockSpec((rows, width), lambda j: (0, 0)),
+        scratch_shapes=[pltpu.VMEM((rows, width), jnp.float32)],
+        compiler_params=pltpu.CompilerParams(
+            dimension_semantics=("arbitrary",), vmem_limit_bytes=32 << 20
+        ),
+        cost_estimate=pl.CostEstimate(
+            flops=8 * rows * (key_count + far_count) * width,
+            bytes_accessed=4 * key_count * width,
+            transcendentals=rows * (key_count + far_count) * HEADS,
+        ),
+    )(
+        ends,
+        query_pos,
+        key_pos,
+        far_pos,
+        queries,
+        keys,
+        values,
+        far_rows,
+        far_rows,
+        o_weight,
+        placed,
+    )
 
 
 def local(
@@ -433,101 +533,42 @@
     arrived_place = jnp.where(tags[:, 2] == 1, tags[:, 0] * 16 + tags[:, 1], tile_rows)
     lands = (order[:, None] == arrived_place[None, :]).astype(jnp.bfloat16)
     placed = jnp.dot(lands, arrived, preferred_element_type=jnp.float32).astype(jnp.bfloat16)
-    start_pos = seq_index * tile_rows
     slide_ends = jnp.cumsum(slide_lengths[0])
 
-    def slides_from(first_pos, count):
-        spots = first_pos + jnp.arange(count, dtype=jnp.int32)
-        return jnp.sum((spots[:, None] >= slide_ends[None, :]).astype(jnp.int32), 1)
-
-    slide_of = slides_from(start_pos, tile_rows)
     seq_resid = placed.astype(jnp.float32)
     span = W_SEG // tile_rows
-    block = jnp.concatenate([placed] + [crossed(placed, r) for r in range(1, span)], 0)
-    normed_seq = layer_norm(block.astype(jnp.float32), attn_gain, attn_bias).astype(jnp.bfloat16)
-    queries = jnp.dot(
-        normed_seq[:tile_rows], q_weight, preferred_element_type=jnp.float32
-    ).astype(jnp.bfloat16)
-    keys_proj = jnp.dot(normed_seq, k_weight, preferred_element_type=jnp.float32).astype(
+    normed_seq = layer_norm(seq_resid, attn_gain, attn_bias).astype(jnp.bfloat16)
+    block = jnp.concatenate(
+        [normed_seq] + [crossed(normed_seq, r) for r in range(1, span)], 0
+    )
+    queries = jnp.dot(normed_seq, q_weight, preferred_element_type=jnp.float32).astype(
         jnp.bfloat16
     )
-    values_proj = jnp.dot(normed_seq, v_weight, preferred_element_type=jnp.float32).astype(
+    keys_proj = jnp.dot(block, k_weight, preferred_element_type=jnp.float32).astype(jnp.bfloat16)
+    values_proj = jnp.dot(block, v_weight, preferred_element_type=jnp.float32).astype(
         jnp.bfloat16
     )
-    scale_factor = HEAD_DIM ** (-0.5)
     chosen = jnp.concatenate([pick_dilated(keys_proj), pick_dilated(values_proj)], 1)
     far_pieces = [chosen] + [
         crossed(chosen, r) for r in range(span, lax.axis_size("seq"), span)
     ]
-    head_q = queries.reshape(tile_rows, HEADS, HEAD_DIM)
-    key_total = span * tile_rows
-    all_keys = keys_proj.reshape(key_total, HEADS, HEAD_DIM)
-    all_values = values_proj.reshape(key_total, HEADS, HEAD_DIM)
-    key_slides = jnp.concatenate(
-        [slides_from((seq_index ^ r) * tile_rows, tile_rows) for r in range(span)]
-    )
-    all_mask = (slide_of[:, None] == key_slides[None, :])[None]
-    scores = (
-        jnp.einsum("qhd,khd->hqk", head_q, all_keys, preferred_element_type=jnp.float32)
-        * scale_factor
-    )
-    row_max = jnp.max(jnp.where(all_mask, scores, -1e30), -1, keepdims=True)
-    weights = jnp.where(all_mask, jnp.exp(scores - row_max), 0.0)
-    denom_sum = jnp.sum(weights, -1)
-    mixed = (
-        jnp.einsum(
-            "hqk,khd->hqd",
-            weights.astype(jnp.bfloat16),
-            all_values,
-            preferred_element_type=jnp.float32,
-        )
-        / denom_sum[..., None]
-    )
-    block_lse = row_max[..., 0] + jnp.log(denom_sum)
-    local_out = jnp.transpose(mixed, (1, 0, 2))
-    local_lse = jnp.transpose(block_lse)
-    picked = tile_rows // RATE
-    selected_query = pick_dilated(queries).reshape(picked, HEADS, HEAD_DIM)
-    query_slide = jnp.transpose(slide_of.reshape(picked, RATE)[:, :HEADS])
     far_rows = jnp.concatenate(far_pieces, 0)
-    key_count = far_rows.shape[0]
-    key_head_rows = far_rows[:, :width].reshape(key_count, HEADS, HEAD_DIM)
-    value_heads = far_rows[:, width:].reshape(key_count, HEADS, HEAD_DIM)
-    far_scores = (
-        jnp.einsum(
-            "tbx,pbx->btp", selected_query, key_head_rows, preferred_element_type=jnp.float32
-        )
-        * scale_factor
-    )
-    key_first = jnp.concatenate(
-        [
-            (seq_index ^ r) * tile_rows + RATE * jnp.arange(picked, dtype=jnp.int32)
-            for r in range(lax.axis_size("seq"))
-        ]
-    )
-    key_pos = key_first[None, :] + jnp.arange(HEADS, dtype=jnp.int32)[:, None]
-    far_allowed = (
-        query_slide[:, :, None]
-        == jnp.sum((key_pos[..., None] >= slide_ends[None, None, :]).astype(jnp.int32), -1)[
-            :, None, :
-        ]
-    )
-    far_max = jnp.max(jnp.where(far_allowed, far_scores, -1e30), -1, keepdims=True)
-    far_weights = jnp.where(far_allowed, jnp.exp(far_scores - far_max), 0.0)
-    far_sum = jnp.sum(far_weights, -1)
-    far_out = (
-        jnp.einsum(
-            "gbr,rga->gba",
-            far_weights.astype(jnp.bfloat16),
-            value_heads,
-            preferred_element_type=jnp.float32,
-        )
-        / far_sum[..., None]
-    )
-    far_lse = far_max[..., 0] + jnp.log(far_sum)
-    attn = combine(local_out, local_lse, far_out, far_lse, tile_rows).astype(jnp.bfloat16)
-    result = (seq_resid + jnp.dot(attn, o_weight, preferred_element_type=jnp.float32)).astype(
-        jnp.bfloat16
+
+    def spots(peers, step):
+        offsets = jnp.arange(0, tile_rows, step, dtype=jnp.int32)
+        return jnp.concatenate([(seq_index ^ r) * tile_rows + offsets for r in peers])
+
+    result = attend(
+        slide_ends,
+        spots([0], 1)[:, None],
+        spots(range(span), 1)[None, :],
+        spots(range(lax.axis_size("seq")), RATE)[None, :],
+        queries,
+        keys_proj,
+        values_proj,
+        far_rows,
+        o_weight,
+        placed,
     )
     return result[None]
 

time: 234 us -> 212 us (0.906)
  local copies, waits for them, and re-layouts: 21.6 us -> 1.08 us
  waiting for transfers between devices: 31.6 us -> 48 us
  matrix products: 26.4 us -> 10.3 us
  other arithmetic: 23.6 us -> 9.93 us
  Pallas kernels: 123 us -> 134 us
    dot_general x8 -> x3, matrix products: 22.5 us -> 6.27 us  [the longest x1 2.91 us: local(): jnp.dot(block, v_weight, preferred_element_type=jnp.float32)]
    ppermute x4, waiting for transfers between devices: 9.04 us -> 25.1 us  [crossed(): lax.ppermute(block, 'seq', [(low, low ^ offset) for low in range(count)])]
    pallas_call x0 -> x1, Pallas kernels: none -> 11.7 us  [attend(): pl.pallas_call(attention_kernel, out_shape=jax.ShapeDtypeStruct((rows, wi...]
    unnamed x54 -> x34, local copies, waits for them, and re-layouts: 5.94 us -> 0.31 us
    reduce_sum x4 -> x0, other arithmetic: 5.56 us -> none  [the longest x1 3.88 us: local(): denom_sum = jnp.sum(weights, -1)]
    convert_element_type x3 -> x0, local copies, waits for them, and re-layouts: 5.46 us -> none  [the longest x1 2.65 us: local(): jnp.dot(normed_seq, v_weight, preferred_element_type=jnp.float32)]
    reshape x4 -> x0, local copies, waits for them, and re-layouts: 3.06 us -> none  [the longest x1 2.77 us: combine(): distant_output_total = jnp.broadcast_to(jnp.transpose(far_out, (1, 0, 2))...]
    convert_element_type x1, other arithmetic: 3.03 us -> 0.25 us  [local(): layer_norm(seq_resid, attn_gain, attn_bias).astype(jnp.bfloat16)]
  transfers between devices with their start and end apart: 5 -> 5, of which waited for: 4 -> 5; matrix products, arithmetic and copies ran while one was open for 8% -> 2% of each run, Pallas kernels for 0% -> 0%
where the time goes in v3:
time: 212 us; the launch traced here: 211 us
  Pallas kernels  134 us (63%)
  waiting for transfers between devices  48 us (23%)
  matrix products  10.3 us (5%)
  other arithmetic  9.93 us (5%)
  starting transfers between devices  7.25 us (3%)
    pallas_call x1, Pallas kernels, ffn_sums(): pl.pallas_call(functools.partial(ffn_kernel, across), out_shape=jax.Shape...  123 us
    ppermute x4, waiting for transfers between devices, crossed(): lax.ppermute(block, 'seq', [(low, low ^ offset) for low in range(count)])  25.1 us
    all_to_all x1, waiting for transfers between devices, local(): lax.all_to_all(outgoing, ('grp', 'seq'), split_axis=0, concat_axis=0, til...  22.8 us
    pallas_call x1, Pallas kernels, attend(): pl.pallas_call(attention_kernel, out_shape=jax.ShapeDtypeStruct((rows, wi...  11.7 us
  transfers between devices with their start and end apart: 5, of which 5 were waited for; matrix products, arithmetic and copies ran while one was open for 2% of the time, Pallas kernels for 0%

profile of v3, /device:TPU:0, one launch (start us, length us, event | category | flops | bytes accessed | tf_op | source)
XLA Modules:
  0.0 211.3 jit_solution(5865525292026616206)
XLA Ops:
  0.0 0.0 copy-start
  0.0 0.0 copy-start.1
  0.0 0.0 copy-start.2
  0.1 1.5 convert_reduce_fusion
  1.5 1.6 fusion.2
  3.1 1.5 fusion.5.normed_ref
  4.7 0.0 copy-start.4
  4.7 0.0 copy-start.7
  4.7 122.7 %shard_map.181 = f32[256,1536]{1,0:T(8,128)S(1)} custom-call(bf16[256,1536]{1,0:T(8,128)(2,1)S(1)} %fusion.5.normed_ref, bf16[512,1536]{1,0:T(8,128)(2,1)S(1)} %copy-done.1, bf16[512,1536]{1,0:T(8,128)(2,1)S(1)} %copy-done.2, bf16[512,1536]{1,0:T(8,128)(2,1)} %down_ref.1), custom_call_target="tpu_custom_call" | custom-call | flops 9663676416 | bytes 4718592 | tf_op jit(solution)/shard_map/pallas_call | solution.py:313
  127.5 0.3 fusion.21
  127.8 0.0 copy-start.13
  127.8 0.0 copy-start.14
  127.8 0.0 copy-start.15
  127.8 0.4 multiply_reduce_fusion
  128.2 0.2 copy-done.12
  128.5 0.2 convert_reduce_fusion.2
  128.7 1.0 fusion.6
  129.7 0.1 add_convert_fusion.2
  129.8 1.4 convolution_convert_fusion.2
  131.2 3.5 %all-to-all-start = ((bf16[32,16,896]{2,1,0:T(8,128)(2,1)}), bf16[32,16,896]{2,1,0:T(8,128)(2,1)}, u32[]{:S(2)}, u32[]{:S(2)}) async-start(bf16[32,16,896]{2,1,0:T(8,128)(2,1)} %bitcast.4), calls=%async_computation | async-start | bytes 1835008 | tf_op jit(solution)/shard_map/all_to_all | solution.py:529
  134.8 0.6 fusion.36
  135.4 0.6 fusion.34
  136.0 0.5 fusion.30
  136.5 22.8 %all-to-all-done = bf16[32,16,896]{2,1,0:T(8,128)(2,1)} async-done(((bf16[32,16,896]{2,1,0:T(8,128)(2,1)}), bf16[32,16,896]{2,1,0:T(8,128)(2,1)}, u32[]{:S(2)}, u32[]{:S(2)}) %all-to-all-start) | async-done | bytes 917536 | tf_op jit(solution)/shard_map/all_to_all | solution.py:529
  159.4 1.0 slice_convert_fusion
  160.3 0.3 fusion.23
  160.6 0.0 copy-start.16
  160.6 1.6 convert_reduce_fusion.1
  162.2 0.2 fusion.9
  162.5 0.3 fusion.12
  162.8 0.8 collective-permute-start
  163.5 0.0 collective-permute-start.1
  163.6 2.8 %collective-permute-start.2 = (bf16[256,768]{1,0:T(8,128)(2,1)S(1)}, bf16[256,768]{1,0:T(8,128)(2,1)}, u32[]{:S(2)}, u32[]{:S(2)}) collective-permute-start(bf16[256,768]{1,0:T(8,128)(2,1)S(1)} %fusion.12), channel_id=1, source_target_pairs={{0,3},{1,2},{2,1},{3,0},{4,7},{5,6},{6,5},{7,4},{8,11},{9,10},{10,... | collective-permute-start | bytes 1179656 | tf_op jit(solution)/shard_map/ppermute | solution.py:18
  166.3 0.6 fusion.32
  166.9 0.2 reduce-window.9
  167.1 0.8 concatenate.19
  167.9 0.0 copy-start.6
  167.9 6.1 %collective-permute-done = bf16[256,768]{1,0:T(8,128)(2,1)S(1)} collective-permute-done((bf16[256,768]{1,0:T(8,128)(2,1)S(1)}, bf16[256,768]{1,0:T(8,128)(2,1)S(1)}, u32[]{:S(2)}, u32[]{:S(2)}) %collective-permute-start) | collective-permute-done | bytes 393248 | tf_op jit(solution)/shard_map/ppermute | solution.py:18
  174.0 1.7 collective-permute-done.1
  175.7 7.6 %collective-permute-done.2 = bf16[256,768]{1,0:T(8,128)(2,1)} collective-permute-done((bf16[256,768]{1,0:T(8,128)(2,1)S(1)}, bf16[256,768]{1,0:T(8,128)(2,1)}, u32[]{:S(2)}, u32[]{:S(2)}) %collective-permute-start.2) | collective-permute-done | bytes 393248 | tf_op jit(solution)/shard_map/ppermute | solution.py:18
  183.3 2.9 %convolution_convert_fusion.value_ref = bf16[1024,768]{1,0:T(8,128)(2,1)S(1)} fusion(bf16[768,768]{1,0:T(8,128)(2,1)} %param.36, bf16[256,768]{1,0:T(8,128)(2,1)} %collective-permute-done.2, bf16[256,768]{1,0:T(8,128)(2,1)} %collective-permute-done.1, bf16[256,768]{1,0:T(8,128)(2,1)S(1)} %collective-permute-done, bf16[256,768]{1,0:T(8,128)(2,1)S(1)} %fusion.12), kind=kOutput, calls=%fused_computation.5 | convolution fusion | flops 1215037440 | bytes 4325376 | tf_op jit(solution)/shard_map/dot_general | solution.py:548
  186.2 0.0 copy-start.5
  186.2 2.9 %select_reduce_fusion.1 = (bf16[64,768]{1,0:T(8,128)(2,1)S(1)}, bf16[64,768]{1,0:T(8,128)(2,1)S(1)}, bf16[1024,768]{1,0:T(8,128)(2,1)S(1)}) fusion(pred[16,768]{1,0:T(8,128)(4,1)S(1)} %iota_compare_fusion.5, bf16[1024,768]{1,0:T(8,128)(2,1)S(1)} %convolution_convert_fusion.value_ref, bf16[768,768]{1,0:T(8,128)(2,1)S(1)} %copy-done.6, ...), kind=kOutput, calls=%fused_computation.13 | convolution fusion | flops 1218084864 | bytes 6107136 | tf_op jit(solution)/shard_map/dot_general | solution.py:547
  189.1 0.0 copy-start.3
  189.1 0.2 collective-permute-start.3
  189.3 0.5 convolution_convert_fusion.3.query_ref
  189.8 9.8 %collective-permute-done.3 = bf16[64,1536]{1,0:T(8,128)(2,1)S(1)} collective-permute-done((bf16[64,1536]{1,0:T(8,128)(2,1)S(1)}, bf16[64,1536]{1,0:T(8,128)(2,1)S(1)}, u32[]{:S(2)}, u32[]{:S(2)}) %collective-permute-start.3) | collective-permute-done | bytes 196640 | tf_op jit(solution)/shard_map/ppermute | solution.py:18
  199.6 11.7 %shard_map.182 = bf16[256,768]{1,0:T(8,128)(2,1)} custom-call(s32[4]{0:T(128)S(1)} %bitcast.18, s32[256,1]{1,0:T(8,128)S(1)} %iota_add_fusion.query_pos_ref, s32[1,1024]{1,0:T(1,128)S(1)} %bitcast.16, s32[1,128]{1,0:T(1,128)S(1)} %bitcast.17, bf16[256,768]{1,0:T(8,128)(2,1)S(1)} %convolution_convert_fusion.3.query_ref, ...), custom_call_target="tpu_custom_call" | custom-call | flops 1811939328 | bytes 3145728 | tf_op jit(solution)/shard_map/pallas_call | solution.py:437
  (39 shorter events, 0.2 us)
Async XLA Ops:
  0.0 128.6 %copy-start = (bf16[1536,768]{1,0:T(8,128)(2,1)S(1)}, bf16[1536,768]{1,0:T(8,128)(2,1)}, u32[]{:S(2)}) copy-start(bf16[1536,768]{1,0:T(8,128)(2,1)} %param.28) | copy-start | bytes 7077892
  0.0 3.1 %copy-start.9 = (f32[1536]{0:T(1024)S(1)}, f32[1536]{0:T(1024)}, u32[]{:S(2)}) copy-start(f32[1536]{0:T(1024)} %param.20) | copy-start | bytes 18436
  0.0 3.1 %copy-start.8 = (f32[1536]{0:T(1024)S(1)}, f32[1536]{0:T(1024)}, u32[]{:S(2)}) copy-start(f32[1536]{0:T(1024)} %param.21) | copy-start | bytes 18436
  0.0 4.6 %copy-start.1 = (bf16[512,1536]{1,0:T(8,128)(2,1)S(1)}, bf16[512,1536]{1,0:T(8,128)(2,1)}, u32[]{:S(2)}) copy-start(bf16[512,1536]{1,0:T(8,128)(2,1)} %gate_ref.1) | copy-start | bytes 4718596
  0.0 4.6 %copy-start.2 = (bf16[512,1536]{1,0:T(8,128)(2,1)S(1)}, bf16[512,1536]{1,0:T(8,128)(2,1)}, u32[]{:S(2)}) copy-start(bf16[512,1536]{1,0:T(8,128)(2,1)} %up_ref.1) | copy-start | bytes 4718596
  4.7 122.8 %copy-start.4 = (bf16[256,1536]{1,0:T(8,128)(2,1)S(1)}, bf16[256,1536]{1,0:T(8,128)(2,1)}, u32[]{:S(2)}) copy-start(bf16[256,1536]{1,0:T(8,128)(2,1)} %param.19) | copy-start | bytes 2359300
  4.7 122.8 %copy-start.7 = (f32[1536]{0:T(1024)S(1)}, f32[1536]{0:T(1024)}, u32[]{:S(2)}) copy-start(f32[1536]{0:T(1024)} %param.25) | copy-start | bytes 18436
  127.8 0.7 copy-start.12
  127.8 0.9 copy-start.13
  127.8 0.9 copy-start.14
  127.8 0.9 copy-start.15
  131.2 28.1 %all-to-all-start = ((bf16[32,16,896]{2,1,0:T(8,128)(2,1)}), bf16[32,16,896]{2,1,0:T(8,128)(2,1)}, u32[]{:S(2)}, u32[]{:S(2)}) async-start(bf16[32,16,896]{2,1,0:T(8,128)(2,1)} %bitcast.4), calls=%async_computation | async-start | bytes 1835008 | tf_op jit(solution)/shard_map/all_to_all | solution.py:529
  159.4 3.1 %copy-start.10 = (f32[768]{0:T(1024)S(1)}, f32[768]{0:T(1024)}, u32[]{:S(2)}) copy-start(f32[768]{0:T(1024)} %param.33) | copy-start | bytes 9220
  159.4 3.2 %copy-start.11 = (f32[768]{0:T(1024)S(1)}, f32[768]{0:T(1024)}, u32[]{:S(2)}) copy-start(f32[768]{0:T(1024)} %param.32) | copy-start | bytes 9220
  160.6 6.3 %copy-start.16 = (s32[1,4]{1,0:T(1,128)S(1)}, s32[1,4]{1,0:T(1,128)}, u32[]{:S(2)}) copy-start(s32[1,4]{1,0:T(1,128)} %param.31) | copy-start | bytes 52
  162.8 11.2 %collective-permute-start = (bf16[256,768]{1,0:T(8,128)(2,1)S(1)}, bf16[256,768]{1,0:T(8,128)(2,1)S(1)}, u32[]{:S(2)}, u32[]{:S(2)}) collective-permute-start(bf16[256,768]{1,0:T(8,128)(2,1)S(1)} %fusion.12), channel_id=1, source_target_pairs={{0,1},{1,0},{2,3},{3,2},{4,5},{5,4},{6,7},{7,6},{8,9},{9,8},{10,11... | collective-permute-start | bytes 1179656 | tf_op jit(solution)/shard_map/ppermute | solution.py:18
  163.5 12.1 %collective-permute-start.1 = (bf16[256,768]{1,0:T(8,128)(2,1)S(1)}, bf16[256,768]{1,0:T(8,128)(2,1)}, u32[]{:S(2)}, u32[]{:S(2)}) collective-permute-start(bf16[256,768]{1,0:T(8,128)(2,1)S(1)} %fusion.12), channel_id=1, source_target_pairs={{0,2},{1,3},{2,0},{3,1},{4,6},{5,7},{6,4},{7,5},{8,10},{9,11},{10,... | collective-permute-start | bytes 1179656 | tf_op jit(solution)/shard_map/ppermute | solution.py:18
  163.6 19.7 %collective-permute-start.2 = (bf16[256,768]{1,0:T(8,128)(2,1)S(1)}, bf16[256,768]{1,0:T(8,128)(2,1)}, u32[]{:S(2)}, u32[]{:S(2)}) collective-permute-start(bf16[256,768]{1,0:T(8,128)(2,1)S(1)} %fusion.12), channel_id=1, source_target_pairs={{0,3},{1,2},{2,1},{3,0},{4,7},{5,6},{6,5},{7,4},{8,11},{9,10},{10,... | collective-permute-start | bytes 1179656 | tf_op jit(solution)/shard_map/ppermute | solution.py:18
  167.9 18.3 %copy-start.6 = (bf16[768,768]{1,0:T(8,128)(2,1)S(1)}, bf16[768,768]{1,0:T(8,128)(2,1)}, u32[]{:S(2)}) copy-start(bf16[768,768]{1,0:T(8,128)(2,1)} %param.35) | copy-start | bytes 3538948
  186.2 3.1 %copy-start.5 = (bf16[768,768]{1,0:T(8,128)(2,1)S(1)}, bf16[768,768]{1,0:T(8,128)(2,1)}, u32[]{:S(2)}) copy-start(bf16[768,768]{1,0:T(8,128)(2,1)} %param.34) | copy-start | bytes 3538948
  189.1 10.5 %copy-start.3 = (bf16[768,768]{1,0:T(8,128)(2,1)S(1)}, bf16[768,768]{1,0:T(8,128)(2,1)}, u32[]{:S(2)}) copy-start(bf16[768,768]{1,0:T(8,128)(2,1)} %o_ref.1) | copy-start | bytes 3538948
  189.1 10.5 %collective-permute-start.3 = (bf16[64,1536]{1,0:T(8,128)(2,1)S(1)}, bf16[64,1536]{1,0:T(8,128)(2,1)S(1)}, u32[]{:S(2)}, u32[]{:S(2)}) collective-permute-start(bf16[64,1536]{1,0:T(8,128)(2,1)S(1)} %pad_maximum_fusion.4), channel_id=1, source_target_pairs={{0,4},{1,5},{2,6},{3,7},{4,0},{5,1},{6,2},{7,3},{8,12},{9,13},{10,... | collective-permute-start | bytes 589832 | tf_op jit(solution)/shard_map/ppermute | solution.py:18

commit v4 on v3

--- a/solution.py
+++ b/solution.py
@@ -145,45 +145,10 @@
         y_copy(r, i).wait_recv()
         twin_copy(r, i, mine).start()
 
-    marks = [len(fetches) // 3, 2 * len(fetches) // 3]
-    done = 0
-    for k in range(1, DEPTH):
-
-        @pl.when(z >= k)
-        def _():
-            hop_right(k).wait_recv()
-
-        if k < DEPTH - 1:
-
-            @pl.when((z >= k) & has_right)
-            def _():
-                hop_right(k + 1).start()
-
-        @pl.when(z <= DEPTH - 1 - k)
-        def _():
-            hop_left(k).wait_recv()
-
-        if k < DEPTH - 1:
-
-            @pl.when((z <= DEPTH - 1 - k) & has_left)
-            def _():
-                hop_left(k + 1).start()
-
-            while done < marks[k - 1]:
-                relay(*fetches[done])
-                done += 1
-    while done < len(fetches):
-        relay(*fetches[done])
-        done += 1
-    for load in loads[1:]:
-        load.wait()
-    for r, i in fetches:
-        twin_copy(r, i, theirs).wait_recv()
-
-    def products(first):
+    def products(spot_of, spot_count, low, high):
         def step(index, carry):
-            spot = first + index // across
-            r = index % across
+            spot = spot_of(index // (high - low))
+            r = low + index % (high - low)
             tile = tiles[spot]
             dims = (((1,), (1,)), ((), ()))
             gate = lax.dot_general(
@@ -205,7 +170,44 @@
 
             return carry
 
-        lax.fori_loop(0, 2 * across, step, 0)
+        lax.fori_loop(0, spot_count * (high - low), step, 0)
+
+    marks = [len(fetches) // 3, 2 * len(fetches) // 3]
+    done = 0
+    for k in range(1, DEPTH):
+
+        @pl.when(z >= k)
+        def _():
+            hop_right(k).wait_recv()
+
+        if k < DEPTH - 1:
+
+            @pl.when((z >= k) & has_right)
+            def _():
+                hop_right(k + 1).start()
+
+        @pl.when(z <= DEPTH - 1 - k)
+        def _():
+            hop_left(k).wait_recv()
+
+        if k < DEPTH - 1:
+
+            @pl.when((z <= DEPTH - 1 - k) & has_left)
+            def _():
+                hop_left(k + 1).start()
+
+            while done < marks[k - 1]:
+                relay(*fetches[done])
+                done += 1
+        if k == DEPTH - 2:
+            for load in loads[1:]:
+                load.wait()
+            products(lambda j: 2 + j, 2, 0, 1)
+    while done < len(fetches):
+        relay(*fetches[done])
+        done += 1
+    for r, i in fetches:
+        twin_copy(r, i, theirs).wait_recv()
 
     def sum_right(t):
         return pltpu.make_async_remote_copy(
@@ -262,9 +264,11 @@
         def _():
             sum_left(t).start()
 
-    products(0)
+    flip = (z >= DEPTH // 2).astype(jnp.int32)
+    products(lambda j: flip, 1, 0, across)
     pass_on(1)
-    products(2)
+    products(lambda j: 2 + j, 2, 1, across)
+    products(lambda j: 1 - flip, 1, 0, across)
     pass_on(2)
     pass_on(3)
 
@@ -538,6 +542,18 @@
     seq_resid = placed.astype(jnp.float32)
     span = W_SEG // tile_rows
     normed_seq = layer_norm(seq_resid, attn_gain, attn_bias).astype(jnp.bfloat16)
+    chosen = jnp.concatenate(
+        [
+            pick_dilated(
+                jnp.dot(normed_seq, weight, preferred_element_type=jnp.float32).astype(
+                    jnp.bfloat16
+                )
+            )
+            for weight in (k_weight, v_weight)
+        ],
+        1,
+    )
+    sent = [crossed(chosen, r) for r in range(span, lax.axis_size("seq"))]
     block = jnp.concatenate(
         [normed_seq] + [crossed(normed_seq, r) for r in range(1, span)], 0
     )
@@ -548,10 +564,8 @@
     values_proj = jnp.dot(block, v_weight, preferred_element_type=jnp.float32).astype(
         jnp.bfloat16
     )
-    chosen = jnp.concatenate([pick_dilated(keys_proj), pick_dilated(values_proj)], 1)
-    far_pieces = [chosen] + [
-        crossed(chosen, r) for r in range(span, lax.axis_size("seq"), span)
-    ]
+    near_chosen = jnp.concatenate([pick_dilated(keys_proj), pick_dilated(values_proj)], 1)
+    far_pieces = [near_chosen] + sent
     far_rows = jnp.concatenate(far_pieces, 0)
 
     def spots(peers, step):

time: 212 us -> 195 us (0.920)
  waiting for transfers between devices: 48 us -> 36.6 us
  starting transfers between devices: 7.25 us -> 11.9 us
  other arithmetic: 9.93 us -> 6.7 us
  Pallas kernels: 134 us -> 131 us
  matrix products: 10.3 us -> 7.67 us
    ppermute x4 -> x7, waiting for transfers between devices: 25.1 us -> 12.4 us  [crossed(): lax.ppermute(block, 'seq', [(low, low ^ offset) for low in range(count)])]
    ppermute x4 -> x7, starting transfers between devices: 3.72 us -> 9.07 us  [crossed(): lax.ppermute(block, 'seq', [(low, low ^ offset) for low in range(count)])]
    pallas_call x1, Pallas kernels: 123 us -> 120 us  [ffn_sums(): pl.pallas_call(functools.partial(ffn_kernel, across), out_shape=jax.Shape...]
    add x7, other arithmetic: 2.31 us -> 0.04 us  [spots(): (seq_index ^ r) * tile_rows + offsets]
  transfers between devices with their start and end apart: 5 -> 8, of which waited for: 5 -> 4; matrix products, arithmetic and copies ran while one was open for 2% -> 3% of each run, Pallas kernels for 0% -> 0%
where the time goes in v4:
time: 195 us
  Pallas kernels  131 us (67%)
  waiting for transfers between devices  36.6 us (19%)
  starting transfers between devices  11.9 us (6%)
  matrix products  7.67 us (4%)
  other arithmetic  6.7 us (3%)
    pallas_call x1, Pallas kernels, ffn_sums(): pl.pallas_call(functools.partial(ffn_kernel, across), out_shape=jax.Shape...  120 us
    all_to_all x1, waiting for transfers between devices, local(): lax.all_to_all(outgoing, ('grp', 'seq'), split_axis=0, concat_axis=0, til...  24.2 us
    ppermute x7, waiting for transfers between devices, crossed(): lax.ppermute(block, 'seq', [(low, low ^ offset) for low in range(count)])  12.4 us
    pallas_call x1, Pallas kernels, attend(): pl.pallas_call(attention_kernel, out_shape=jax.ShapeDtypeStruct((rows, wi...  11.7 us
    ppermute x7, starting transfers between devices, crossed(): lax.ppermute(block, 'seq', [(low, low ^ offset) for low in range(count)])  9.07 us
  transfers between devices with their start and end apart: 8, of which 4 were waited for; matrix products, arithmetic and copies ran while one was open for 3% of the time, Pallas kernels for 0%

profile of v4, /device:TPU:0, one launch (start us, length us, event | category | flops | bytes accessed | tf_op | source)
XLA Modules:
  0.0 195.0 jit_solution(6119269426948867396)
XLA Ops:
  0.0 0.0 copy-start.1
  0.0 0.0 copy-start.2
  0.1 1.5 convert_reduce_fusion
  1.5 1.6 fusion.2
  3.1 1.5 fusion.5.normed_ref
  4.7 0.0 copy-start.4
  4.7 0.0 copy-start.8
  4.7 119.5 %shard_map.181 = f32[256,1536]{1,0:T(8,128)S(1)} custom-call(bf16[256,1536]{1,0:T(8,128)(2,1)S(1)} %fusion.5.normed_ref, bf16[512,1536]{1,0:T(8,128)(2,1)S(1)} %copy-done.1, bf16[512,1536]{1,0:T(8,128)(2,1)S(1)} %copy-done.2, bf16[512,1536]{1,0:T(8,128)(2,1)} %down_ref.1), custom_call_target="tpu_custom_call" | custom-call | flops 9663676416 | bytes 4718592 | tf_op jit(solution)/shard_map/pallas_call | solution.py:317
  124.2 0.3 fusion.21
  124.5 0.0 copy-start.14
  124.5 0.0 copy-start.15
  124.5 0.0 copy-start.16
  124.6 0.4 multiply_reduce_fusion
  125.0 0.2 copy-done.13
  125.2 0.2 convert_reduce_fusion.2
  125.4 1.0 fusion.6
  126.4 0.1 add_convert_fusion.2
  126.6 0.0 copy-start.17
  126.6 1.4 convolution_convert_fusion.2
  128.0 2.8 %all-to-all-start = ((bf16[32,16,896]{2,1,0:T(8,128)(2,1)}), bf16[32,16,896]{2,1,0:T(8,128)(2,1)S(1)}, u32[]{:S(2)}, u32[]{:S(2)}) async-start(bf16[32,16,896]{2,1,0:T(8,128)(2,1)} %bitcast.29), calls=%async_computation | async-start | bytes 1835008 | tf_op jit(solution)/shard_map/all_to_all | solution.py:533
  130.8 0.2 reduce-window.9
  131.0 0.1 concatenate.22
  131.2 24.2 %all-to-all-done = bf16[32,16,896]{2,1,0:T(8,128)(2,1)S(1)} async-done(((bf16[32,16,896]{2,1,0:T(8,128)(2,1)}), bf16[32,16,896]{2,1,0:T(8,128)(2,1)S(1)}, u32[]{:S(2)}, u32[]{:S(2)}) %all-to-all-start) | async-done | bytes 917536 | tf_op jit(solution)/shard_map/all_to_all | solution.py:533
  155.4 0.3 fusion.23
  155.7 0.0 copy-start.7
  155.7 0.5 convert_reduce_fusion.1
  156.2 0.0 copy-start.5
  156.2 0.2 fusion.9
  156.5 0.3 fusion.12
  156.8 0.0 copy-start.6
  156.8 0.8 collective-permute-start
  157.5 2.8 %collective-permute-start.2 = (bf16[256,768]{1,0:T(8,128)(2,1)S(1)}, bf16[256,768]{1,0:T(8,128)(2,1)S(1)}, u32[]{:S(2)}, u32[]{:S(2)}) collective-permute-start(bf16[256,768]{1,0:T(8,128)(2,1)S(1)} %fusion.12), channel_id=1, source_target_pairs={{0,3},{1,2},{2,1},{3,0},{4,7},{5,6},{6,5},{7,4},{8,11},{9,10},{10,... | collective-permute-start | bytes 1179656 | tf_op jit(solution)/shard_map/ppermute | solution.py:18
  160.3 0.5 convolution_convert_fusion.3
  160.8 0.5 select_reduce_fusion.3
  161.4 0.1 collective-permute-start.3
  161.4 3.1 %collective-permute-start.4 = (bf16[16,1536]{1,0:T(8,128)(2,1)S(1)}, bf16[16,1536]{1,0:T(8,128)(2,1)S(1)}, u32[]{:S(2)}, u32[]{:S(2)}) collective-permute-start(bf16[16,1536]{1,0:T(8,128)(2,1)S(1)} %pad_maximum_fusion.3), channel_id=1, source_target_pairs={{0,5},{1,4},{2,7},{3,6},{4,1},{5,0},{6,3},{7,2},{8,13},{9,12},{10,... | collective-permute-start | bytes 147464 | tf_op jit(solution)/shard_map/ppermute | solution.py:18
  164.5 0.5 convolution_convert_fusion.5.query_ref
  165.0 3.6 %collective-permute-done = bf16[256,768]{1,0:T(8,128)(2,1)S(1)} collective-permute-done((bf16[256,768]{1,0:T(8,128)(2,1)S(1)}, bf16[256,768]{1,0:T(8,128)(2,1)S(1)}, u32[]{:S(2)}, u32[]{:S(2)}) %collective-permute-start) | collective-permute-done | bytes 393248 | tf_op jit(solution)/shard_map/ppermute | solution.py:18
  168.6 0.7 collective-permute-start.5
  169.3 2.3 %collective-permute-done.1 = bf16[256,768]{1,0:T(8,128)(2,1)S(1)} collective-permute-done((bf16[256,768]{1,0:T(8,128)(2,1)S(1)}, bf16[256,768]{1,0:T(8,128)(2,1)S(1)}, u32[]{:S(2)}, u32[]{:S(2)}) %collective-permute-start.1) | collective-permute-done | bytes 393248 | tf_op jit(solution)/shard_map/ppermute | solution.py:18
  171.7 1.7 collective-permute-start.6
  173.3 6.5 %collective-permute-done.2 = bf16[256,768]{1,0:T(8,128)(2,1)S(1)} collective-permute-done((bf16[256,768]{1,0:T(8,128)(2,1)S(1)}, bf16[256,768]{1,0:T(8,128)(2,1)S(1)}, u32[]{:S(2)}, u32[]{:S(2)}) %collective-permute-start.2) | collective-permute-done | bytes 393248 | tf_op jit(solution)/shard_map/ppermute | solution.py:18
  179.8 1.4 convolution_convert_fusion.value_ref
  181.2 0.0 copy-start.3
  181.2 2.0 %select_reduce_fusion.1 = (bf16[64,768]{1,0:T(8,128)(2,1)S(1)}, bf16[64,768]{1,0:T(8,128)(2,1)S(1)}, bf16[1024,768]{1,0:T(8,128)(2,1)S(1)}) fusion(pred[16,768]{1,0:T(8,128)(4,1)S(1)} %iota_compare_fusion.5, bf16[1024,768]{1,0:T(8,128)(2,1)S(1)} %convolution_convert_fusion.value_ref, bf16[768,768]{1,0:T(8,128)(2,1)S(1)} %copy-done.5, ...), kind=kOutput, calls=%fused_computation.13 | convolution fusion | flops 1218084864 | bytes 6107136 | tf_op jit(solution)/shard_map/dot_general | solution.py:563
  183.2 0.0 collective-permute-done.4
  183.3 0.0 collective-permute-done.6
  183.3 11.7 %shard_map.182 = bf16[256,768]{1,0:T(8,128)(2,1)} custom-call(s32[4]{0:T(128)S(1)} %bitcast.26, s32[256,1]{1,0:T(8,128)S(1)} %iota_add_fusion.query_pos_ref, s32[1,1024]{1,0:T(1,128)S(1)} %bitcast.24, s32[1,128]{1,0:T(1,128)S(1)} %bitcast.25, bf16[256,768]{1,0:T(8,128)(2,1)S(1)} %convolution_convert_fusion.5.query_ref, ...), custom_call_target="tpu_custom_call" | custom-call | flops 1811939328 | bytes 3145728 | tf_op jit(solution)/shard_map/pallas_call | solution.py:441
  (53 shorter events, 0.3 us)
Async XLA Ops:
  0.0 125.4 %copy-start = (bf16[1536,768]{1,0:T(8,128)(2,1)S(1)}, bf16[1536,768]{1,0:T(8,128)(2,1)}, u32[]{:S(2)}) copy-start(bf16[1536,768]{1,0:T(8,128)(2,1)} %param.28) | copy-start | bytes 7077892
  0.0 3.1 %copy-start.10 = (f32[1536]{0:T(1024)S(1)}, f32[1536]{0:T(1024)}, u32[]{:S(2)}) copy-start(f32[1536]{0:T(1024)} %param.20) | copy-start | bytes 18436
  0.0 3.1 %copy-start.9 = (f32[1536]{0:T(1024)S(1)}, f32[1536]{0:T(1024)}, u32[]{:S(2)}) copy-start(f32[1536]{0:T(1024)} %param.21) | copy-start | bytes 18436
  0.0 4.6 %copy-start.1 = (bf16[512,1536]{1,0:T(8,128)(2,1)S(1)}, bf16[512,1536]{1,0:T(8,128)(2,1)}, u32[]{:S(2)}) copy-start(bf16[512,1536]{1,0:T(8,128)(2,1)} %gate_ref.1) | copy-start | bytes 4718596
  0.0 4.6 %copy-start.2 = (bf16[512,1536]{1,0:T(8,128)(2,1)S(1)}, bf16[512,1536]{1,0:T(8,128)(2,1)}, u32[]{:S(2)}) copy-start(bf16[512,1536]{1,0:T(8,128)(2,1)} %up_ref.1) | copy-start | bytes 4718596
  4.7 119.5 %copy-start.4 = (bf16[256,1536]{1,0:T(8,128)(2,1)S(1)}, bf16[256,1536]{1,0:T(8,128)(2,1)}, u32[]{:S(2)}) copy-start(bf16[256,1536]{1,0:T(8,128)(2,1)} %param.19) | copy-start | bytes 2359300
  4.7 119.5 %copy-start.8 = (f32[1536]{0:T(1024)S(1)}, f32[1536]{0:T(1024)}, u32[]{:S(2)}) copy-start(f32[1536]{0:T(1024)} %param.25) | copy-start | bytes 18436
  124.5 0.7 copy-start.13
  124.5 0.9 copy-start.14
  124.5 0.9 copy-start.15
  124.5 0.9 copy-start.16
  126.6 4.2 %copy-start.17 = (s32[1,4]{1,0:T(1,128)S(1)}, s32[1,4]{1,0:T(1,128)}, u32[]{:S(2)}) copy-start(s32[1,4]{1,0:T(1,128)} %param.31) | copy-start | bytes 52
  128.0 27.4 %all-to-all-start = ((bf16[32,16,896]{2,1,0:T(8,128)(2,1)}), bf16[32,16,896]{2,1,0:T(8,128)(2,1)S(1)}, u32[]{:S(2)}, u32[]{:S(2)}) async-start(bf16[32,16,896]{2,1,0:T(8,128)(2,1)} %bitcast.29), calls=%async_computation | async-start | bytes 1835008 | tf_op jit(solution)/shard_map/all_to_all | solution.py:533
  155.4 1.1 copy-start.11
  155.4 1.1 copy-start.12
  155.7 4.6 %copy-start.7 = (bf16[768,768]{1,0:T(8,128)(2,1)S(1)}, bf16[768,768]{1,0:T(8,128)(2,1)}, u32[]{:S(2)}) copy-start(bf16[768,768]{1,0:T(8,128)(2,1)} %param.36) | copy-start | bytes 3538948
  156.2 4.6 %copy-start.5 = (bf16[768,768]{1,0:T(8,128)(2,1)S(1)}, bf16[768,768]{1,0:T(8,128)(2,1)}, u32[]{:S(2)}) copy-start(bf16[768,768]{1,0:T(8,128)(2,1)} %param.35) | copy-start | bytes 3538948
  156.8 7.7 %copy-start.6 = (bf16[768,768]{1,0:T(8,128)(2,1)S(1)}, bf16[768,768]{1,0:T(8,128)(2,1)}, u32[]{:S(2)}) copy-start(bf16[768,768]{1,0:T(8,128)(2,1)} %param.34) | copy-start | bytes 3538948
  156.8 11.8 %collective-permute-start = (bf16[256,768]{1,0:T(8,128)(2,1)S(1)}, bf16[256,768]{1,0:T(8,128)(2,1)S(1)}, u32[]{:S(2)}, u32[]{:S(2)}) collective-permute-start(bf16[256,768]{1,0:T(8,128)(2,1)S(1)} %fusion.12), channel_id=1, source_target_pairs={{0,1},{1,0},{2,3},{3,2},{4,5},{5,4},{6,7},{7,6},{8,9},{9,8},{10,11... | collective-permute-start | bytes 1179656 | tf_op jit(solution)/shard_map/ppermute | solution.py:18
  157.5 14.1 %collective-permute-start.1 = (bf16[256,768]{1,0:T(8,128)(2,1)S(1)}, bf16[256,768]{1,0:T(8,128)(2,1)S(1)}, u32[]{:S(2)}, u32[]{:S(2)}) collective-permute-start(bf16[256,768]{1,0:T(8,128)(2,1)S(1)} %fusion.12), channel_id=1, source_target_pairs={{0,2},{1,3},{2,0},{3,1},{4,6},{5,7},{6,4},{7,5},{8,10},{9,11},{10,... | collective-permute-start | bytes 1179656 | tf_op jit(solution)/shard_map/ppermute | solution.py:18
  157.5 22.2 %collective-permute-start.2 = (bf16[256,768]{1,0:T(8,128)(2,1)S(1)}, bf16[256,768]{1,0:T(8,128)(2,1)S(1)}, u32[]{:S(2)}, u32[]{:S(2)}) collective-permute-start(bf16[256,768]{1,0:T(8,128)(2,1)S(1)} %fusion.12), channel_id=1, source_target_pairs={{0,3},{1,2},{2,1},{3,0},{4,7},{5,6},{6,5},{7,4},{8,11},{9,10},{10,... | collective-permute-start | bytes 1179656 | tf_op jit(solution)/shard_map/ppermute | solution.py:18
  161.4 21.8 %collective-permute-start.3 = (bf16[16,1536]{1,0:T(8,128)(2,1)S(1)}, bf16[16,1536]{1,0:T(8,128)(2,1)S(1)}, u32[]{:S(2)}, u32[]{:S(2)}) collective-permute-start(bf16[16,1536]{1,0:T(8,128)(2,1)S(1)} %pad_maximum_fusion.3), channel_id=1, source_target_pairs={{0,4},{1,5},{2,6},{3,7},{4,0},{5,1},{6,2},{7,3},{8,12},{9,13},{10,... | collective-permute-start | bytes 147464 | tf_op jit(solution)/shard_map/ppermute | solution.py:18
  161.4 21.8 %collective-permute-start.4 = (bf16[16,1536]{1,0:T(8,128)(2,1)S(1)}, bf16[16,1536]{1,0:T(8,128)(2,1)S(1)}, u32[]{:S(2)}, u32[]{:S(2)}) collective-permute-start(bf16[16,1536]{1,0:T(8,128)(2,1)S(1)} %pad_maximum_fusion.3), channel_id=1, source_target_pairs={{0,5},{1,4},{2,7},{3,6},{4,1},{5,0},{6,3},{7,2},{8,13},{9,12},{10,... | collective-permute-start | bytes 147464 | tf_op jit(solution)/shard_map/ppermute | solution.py:18
  168.6 14.6 %collective-permute-start.5 = (bf16[16,1536]{1,0:T(8,128)(2,1)S(1)}, bf16[16,1536]{1,0:T(8,128)(2,1)S(1)}, u32[]{:S(2)}, u32[]{:S(2)}) collective-permute-start(bf16[16,1536]{1,0:T(8,128)(2,1)S(1)} %pad_maximum_fusion.3), channel_id=1, source_target_pairs={{0,6},{1,7},{2,4},{3,5},{4,2},{5,3},{6,0},{7,1},{8,14},{9,15},{10,... | collective-permute-start | bytes 147464 | tf_op jit(solution)/shard_map/ppermute | solution.py:18
  171.7 11.6 %collective-permute-start.6 = (bf16[16,1536]{1,0:T(8,128)(2,1)S(1)}, bf16[16,1536]{1,0:T(8,128)(2,1)S(1)}, u32[]{:S(2)}, u32[]{:S(2)}) collective-permute-start(bf16[16,1536]{1,0:T(8,128)(2,1)S(1)} %pad_maximum_fusion.3), channel_id=1, source_target_pairs={{0,7},{1,6},{2,5},{3,4},{4,3},{5,2},{6,1},{7,0},{8,15},{9,14},{10,... | collective-permute-start | bytes 147464 | tf_op jit(solution)/shard_map/ppermute | solution.py:18
  181.2 2.1 %copy-start.3 = (bf16[768,768]{1,0:T(8,128)(2,1)S(1)}, bf16[768,768]{1,0:T(8,128)(2,1)}, u32[]{:S(2)}) copy-start(bf16[768,768]{1,0:T(8,128)(2,1)} %o_ref.1) | copy-start | bytes 3538948

commit v5 on v4

--- a/solution.py
+++ b/solution.py
@@ -24,7 +24,9 @@
 
 def ffn_kernel(
     across,
-    normed_ref,
+    tile_ref,
+    gain_ref,
+    bias_ref,
     gate_ref,
     up_ref,
     down_ref,
@@ -78,17 +80,18 @@
         pl.semaphore_signal(barrier, inc=1, device_id=y_peer(r))
     pl.semaphore_signal(barrier, inc=1, device_id={"grp": twin})
 
-    loads = [pltpu.make_async_copy(normed_ref, tiles.at[SPOT[0]], local_sem.at[3])]
-    loads += [
+    loads = [
         pltpu.make_async_copy(own[i], weights.at[0, i], local_sem.at[i]) for i in range(3)
     ]
     for load in loads:
         load.start()
+    tiles[SPOT[0]] = layer_norm(
+        tile_ref[...].astype(jnp.float32), gain_ref[...], bias_ref[...]
+    ).astype(jnp.bfloat16)
     pl.semaphore_wait(
         barrier,
         across + has_right.astype(jnp.int32) + has_left.astype(jnp.int32),
     )
-    loads[0].wait()
 
     def hop_right(k):
         return pltpu.make_async_remote_copy(
@@ -200,7 +203,7 @@
                 relay(*fetches[done])
                 done += 1
         if k == DEPTH - 2:
-            for load in loads[1:]:
+            for load in loads:
                 load.wait()
             products(lambda j: 2 + j, 2, 0, 1)
     while done < len(fetches):
@@ -307,9 +310,9 @@
         twin_copy(r, i, mine).wait_send()
 
 
-def ffn_sums(normed, gate_weight, up_weight, down_weight):
+def ffn_sums(tile_cls, gain, bias, gate_weight, up_weight, down_weight):
     across = lax.axis_size("seq") // DEPTH
-    rows, width = normed.shape
+    rows, width = tile_cls.shape
     count = gate_weight.shape[0]
     messages = pltpu.VMEM((DEPTH - 1, rows, width), jnp.bfloat16)
     sem = pltpu.SemaphoreType.DMA
@@ -317,7 +320,8 @@
     return pl.pallas_call(
         functools.partial(ffn_kernel, across),
         out_shape=jax.ShapeDtypeStruct((rows, width), jnp.float32),
-        in_specs=[pl.BlockSpec(memory_space=pl.ANY)] * 4,
+        in_specs=[pl.BlockSpec(memory_space=pltpu.VMEM)] * 3
+        + [pl.BlockSpec(memory_space=pl.ANY)] * 3,
         out_specs=pl.BlockSpec(memory_space=pltpu.VMEM),
         scratch_shapes=[
             pltpu.VMEM((DEPTH, rows, width), jnp.bfloat16),
@@ -327,7 +331,7 @@
             messages,
             messages,
             messages,
-            sem((4,)),
+            sem((3,)),
             sem((2, DEPTH - 1)),
             sem((DEPTH - 1,)),
             sem((across, 3)),
@@ -345,7 +349,7 @@
         cost_estimate=pl.CostEstimate(
             flops=flops, bytes_accessed=6 * count * width, transcendentals=0
         ),
-    )(normed, gate_weight, up_weight, down_weight)
+    )(tile_cls, gain[None], bias[None], gate_weight, up_weight, down_weight)
 
 
 def layer_norm(values, gain_vec, bias_vector):
@@ -504,9 +508,8 @@
     tile_rows = tile_cls.shape[0]
     width = proj_weight.shape[1]
     residual = tile_cls.astype(jnp.float32)
-    normed = layer_norm(residual, ln_gain, ln_bias).astype(jnp.bfloat16)
     seq_index = lax.axis_index("seq")
-    mlp_out = ffn_sums(normed, gate_weight, up_weight, down_weight)
+    mlp_out = ffn_sums(tile_cls, ln_gain, ln_bias, gate_weight, up_weight, down_weight)
     tile_out = residual + layer_scale * mlp_out
     final = layer_norm(tile_out, final_gain, final_bias).astype(jnp.bfloat16)
     embed = (jnp.dot(final, proj_weight, preferred_element_type=jnp.float32) + proj_bias).astype(

time: 195 us -> 196 us (level)
  local copies, waits for them, and re-layouts: 0.42 us -> 5.62 us
  other arithmetic: 6.7 us -> 2.97 us
    unnamed x39 -> x33, local copies, waits for them, and re-layouts: 0.34 us -> 4.13 us
where the time goes in v5:
time: 196 us
  Pallas kernels  131 us (67%)
  waiting for transfers between devices  36.6 us (19%)
  starting transfers between devices  11.9 us (6%)
  matrix products  7.67 us (4%)
  local copies, waits for them, and re-layouts  5.62 us (3%)
  other arithmetic  2.97 us (2%)
    pallas_call x1, Pallas kernels, ffn_sums(): pl.pallas_call(functools.partial(ffn_kernel, across), out_shape=jax.Shape...  119 us
    all_to_all x1, waiting for transfers between devices, local(): lax.all_to_all(outgoing, ('grp', 'seq'), split_axis=0, concat_axis=0, til...  24.2 us
    ppermute x7, waiting for transfers between devices, crossed(): lax.ppermute(block, 'seq', [(low, low ^ offset) for low in range(count)])  12.4 us
    pallas_call x1, Pallas kernels, attend(): pl.pallas_call(attention_kernel, out_shape=jax.ShapeDtypeStruct((rows, wi...  11.7 us
    ppermute x7, starting transfers between devices, crossed(): lax.ppermute(block, 'seq', [(low, low ^ offset) for low in range(count)])  9.08 us
    unnamed x33, local copies, waits for them, and re-layouts  4.13 us
  transfers between devices with their start and end apart: 8, of which 4 were waited for; matrix products, arithmetic and copies ran while one was open for 3% of the time, Pallas kernels for 0%

profile of v5, /device:TPU:0, one launch (start us, length us, event | category | flops | bytes accessed | tf_op | source)
XLA Modules:
  0.0 196.0 jit_solution(9014470841988035678)
XLA Ops:
  0.0 0.8 and_select_fusion.1
  0.9 0.2 convert_reduce_fusion.1
  1.0 0.7 broadcast_in_dim.127.gain_ref
  1.8 0.7 broadcast_in_dim.128.bias_ref
  2.5 1.1 copy-done.1
  3.6 1.4 copy-done.2
  5.0 1.4 copy-done.3
  6.4 119.2 %shard_map.181 = f32[256,1536]{1,0:T(8,128)S(1)} custom-call(bf16[256,1536]{1,0:T(8,128)(2,1)S(1)} %copy-done.1, f32[1,1536]{1,0:T(1,128)S(1)} %broadcast_in_dim.127.gain_ref, f32[1,1536]{1,0:T(1,128)S(1)} %broadcast_in_dim.128.bias_ref, bf16[512,1536]{1,0:T(8,128)(2,1)S(1)} %copy-done.2, bf16[512,1536]{1,0:T(8,128)(2,1)S(1)} %copy-done.3, ...), custom_call_target="tpu_custom_call" | custom-call | flops 9663676416 | bytes 4718592 | tf_op jit(solution)/shard_map/pallas_call | solution.py:320
  125.6 0.3 fusion.15
  125.9 0.0 copy-start.12
  125.9 0.0 copy-start.13
  125.9 0.4 multiply_reduce_fusion
  126.4 0.1 add_convert_fusion.2
  126.5 0.1 copy-done.11
  126.6 0.0 copy-done.12
  126.6 0.0 copy-done.13
  126.6 1.0 fusion
  127.6 0.0 copy-start.14
  127.6 1.4 convolution_convert_fusion.2
  129.0 2.8 %all-to-all-start = ((bf16[32,16,896]{2,1,0:T(8,128)(2,1)}), bf16[32,16,896]{2,1,0:T(8,128)(2,1)S(1)}, u32[]{:S(2)}, u32[]{:S(2)}) async-start(bf16[32,16,896]{2,1,0:T(8,128)(2,1)} %bitcast.29), calls=%async_computation | async-start | bytes 1835008 | tf_op jit(solution)/shard_map/all_to_all | solution.py:536
  131.9 0.2 reduce-window.9
  132.1 0.1 concatenate.22
  132.2 24.2 %all-to-all-done = bf16[32,16,896]{2,1,0:T(8,128)(2,1)S(1)} async-done(((bf16[32,16,896]{2,1,0:T(8,128)(2,1)}), bf16[32,16,896]{2,1,0:T(8,128)(2,1)S(1)}, u32[]{:S(2)}, u32[]{:S(2)}) %all-to-all-start) | async-done | bytes 917536 | tf_op jit(solution)/shard_map/all_to_all | solution.py:536
  156.5 0.3 fusion.17
  156.8 0.0 copy-start.7
  156.8 0.5 convert_reduce_fusion
  157.2 0.0 copy-start.5
  157.3 0.2 fusion.3
  157.5 0.3 fusion.6
  157.8 0.0 copy-start.6
  157.8 0.8 collective-permute-start
  158.6 0.0 collective-permute-start.1
  158.6 2.8 %collective-permute-start.2 = (bf16[256,768]{1,0:T(8,128)(2,1)S(1)}, bf16[256,768]{1,0:T(8,128)(2,1)S(1)}, u32[]{:S(2)}, u32[]{:S(2)}) collective-permute-start(bf16[256,768]{1,0:T(8,128)(2,1)S(1)} %fusion.6), channel_id=1, source_target_pairs={{0,3},{1,2},{2,1},{3,0},{4,7},{5,6},{6,5},{7,4},{8,11},{9,10},{10,... | collective-permute-start | bytes 1179656 | tf_op jit(solution)/shard_map/ppermute | solution.py:18
  161.4 0.5 convolution_convert_fusion.3
  161.9 0.5 select_reduce_fusion.3
  162.4 0.1 collective-permute-start.3
  162.5 3.0 %collective-permute-start.4 = (bf16[16,1536]{1,0:T(8,128)(2,1)S(1)}, bf16[16,1536]{1,0:T(8,128)(2,1)S(1)}, u32[]{:S(2)}, u32[]{:S(2)}) collective-permute-start(bf16[16,1536]{1,0:T(8,128)(2,1)S(1)} %pad_maximum_fusion.3), channel_id=1, source_target_pairs={{0,5},{1,4},{2,7},{3,6},{4,1},{5,0},{6,3},{7,2},{8,13},{9,12},{10,... | collective-permute-start | bytes 147464 | tf_op jit(solution)/shard_map/ppermute | solution.py:18
  165.5 0.5 convolution_convert_fusion.5.query_ref
  166.0 3.6 %collective-permute-done = bf16[256,768]{1,0:T(8,128)(2,1)S(1)} collective-permute-done((bf16[256,768]{1,0:T(8,128)(2,1)S(1)}, bf16[256,768]{1,0:T(8,128)(2,1)S(1)}, u32[]{:S(2)}, u32[]{:S(2)}) %collective-permute-start) | collective-permute-done | bytes 393248 | tf_op jit(solution)/shard_map/ppermute | solution.py:18
  169.6 0.8 collective-permute-start.5
  170.4 2.3 %collective-permute-done.1 = bf16[256,768]{1,0:T(8,128)(2,1)S(1)} collective-permute-done((bf16[256,768]{1,0:T(8,128)(2,1)S(1)}, bf16[256,768]{1,0:T(8,128)(2,1)S(1)}, u32[]{:S(2)}, u32[]{:S(2)}) %collective-permute-start.1) | collective-permute-done | bytes 393248 | tf_op jit(solution)/shard_map/ppermute | solution.py:18
  172.7 1.7 collective-permute-start.6
  174.3 6.4 %collective-permute-done.2 = bf16[256,768]{1,0:T(8,128)(2,1)S(1)} collective-permute-done((bf16[256,768]{1,0:T(8,128)(2,1)S(1)}, bf16[256,768]{1,0:T(8,128)(2,1)S(1)}, u32[]{:S(2)}, u32[]{:S(2)}) %collective-permute-start.2) | collective-permute-done | bytes 393248 | tf_op jit(solution)/shard_map/ppermute | solution.py:18
  180.8 1.4 convolution_convert_fusion.value_ref
  182.2 0.0 copy-start.4
  182.2 2.0 %select_reduce_fusion.1 = (bf16[64,768]{1,0:T(8,128)(2,1)S(1)}, bf16[64,768]{1,0:T(8,128)(2,1)S(1)}, bf16[1024,768]{1,0:T(8,128)(2,1)S(1)}) fusion(pred[16,768]{1,0:T(8,128)(4,1)S(1)} %iota_compare_fusion.5, bf16[1024,768]{1,0:T(8,128)(2,1)S(1)} %convolution_convert_fusion.value_ref, bf16[768,768]{1,0:T(8,128)(2,1)S(1)} %copy-done.5, ...), kind=kOutput, calls=%fused_computation.4 | convolution fusion | flops 1218084864 | bytes 6107136 | tf_op jit(solution)/shard_map/dot_general | solution.py:566
  184.2 0.0 collective-permute-done.3
  184.3 11.7 %shard_map.182 = bf16[256,768]{1,0:T(8,128)(2,1)} custom-call(s32[4]{0:T(128)S(1)} %bitcast.26, s32[256,1]{1,0:T(8,128)S(1)} %iota_add_fusion.query_pos_ref, s32[1,1024]{1,0:T(1,128)S(1)} %bitcast.24, s32[1,128]{1,0:T(1,128)S(1)} %bitcast.25, bf16[256,768]{1,0:T(8,128)(2,1)S(1)} %convolution_convert_fusion.5.query_ref, ...), custom_call_target="tpu_custom_call" | custom-call | flops 1811939328 | bytes 3145728 | tf_op jit(solution)/shard_map/pallas_call | solution.py:445
  (44 shorter events, 0.2 us)
Async XLA Ops:
  0.0 126.5 %copy-start = (bf16[1536,768]{1,0:T(8,128)(2,1)S(1)}, bf16[1536,768]{1,0:T(8,128)(2,1)}, u32[]{:S(2)}) copy-start(bf16[1536,768]{1,0:T(8,128)(2,1)} %param.28) | copy-start | bytes 7077892
  2.5 1.1 copy-start.1
  3.6 1.4 copy-start.2
  5.0 1.4 copy-start.3
  6.4 119.2 %copy-start.8 = (f32[1536]{0:T(1024)S(1)}, f32[1536]{0:T(1024)}, u32[]{:S(2)}) copy-start(f32[1536]{0:T(1024)} %param.25) | copy-start | bytes 18436
  125.9 0.7 copy-start.11
  125.9 0.7 copy-start.12
  125.9 0.7 copy-start.13
  127.6 4.2 %copy-start.14 = (s32[1,4]{1,0:T(1,128)S(1)}, s32[1,4]{1,0:T(1,128)}, u32[]{:S(2)}) copy-start(s32[1,4]{1,0:T(1,128)} %param.31) | copy-start | bytes 52
  129.0 27.4 %all-to-all-start = ((bf16[32,16,896]{2,1,0:T(8,128)(2,1)}), bf16[32,16,896]{2,1,0:T(8,128)(2,1)S(1)}, u32[]{:S(2)}, u32[]{:S(2)}) async-start(bf16[32,16,896]{2,1,0:T(8,128)(2,1)} %bitcast.29), calls=%async_computation | async-start | bytes 1835008 | tf_op jit(solution)/shard_map/all_to_all | solution.py:536
  156.4 1.1 copy-start.9
  156.4 1.1 copy-start.10
  156.8 4.6 %copy-start.7 = (bf16[768,768]{1,0:T(8,128)(2,1)S(1)}, bf16[768,768]{1,0:T(8,128)(2,1)}, u32[]{:S(2)}) copy-start(bf16[768,768]{1,0:T(8,128)(2,1)} %param.36) | copy-start | bytes 3538948
  157.2 4.6 %copy-start.5 = (bf16[768,768]{1,0:T(8,128)(2,1)S(1)}, bf16[768,768]{1,0:T(8,128)(2,1)}, u32[]{:S(2)}) copy-start(bf16[768,768]{1,0:T(8,128)(2,1)} %param.35) | copy-start | bytes 3538948
  157.8 7.7 %copy-start.6 = (bf16[768,768]{1,0:T(8,128)(2,1)S(1)}, bf16[768,768]{1,0:T(8,128)(2,1)}, u32[]{:S(2)}) copy-start(bf16[768,768]{1,0:T(8,128)(2,1)} %param.34) | copy-start | bytes 3538948
  157.8 11.8 %collective-permute-start = (bf16[256,768]{1,0:T(8,128)(2,1)S(1)}, bf16[256,768]{1,0:T(8,128)(2,1)S(1)}, u32[]{:S(2)}, u32[]{:S(2)}) collective-permute-start(bf16[256,768]{1,0:T(8,128)(2,1)S(1)} %fusion.6), channel_id=1, source_target_pairs={{0,1},{1,0},{2,3},{3,2},{4,5},{5,4},{6,7},{7,6},{8,9},{9,8},{10,11... | collective-permute-start | bytes 1179656 | tf_op jit(solution)/shard_map/ppermute | solution.py:18
  158.6 14.1 %collective-permute-start.1 = (bf16[256,768]{1,0:T(8,128)(2,1)S(1)}, bf16[256,768]{1,0:T(8,128)(2,1)S(1)}, u32[]{:S(2)}, u32[]{:S(2)}) collective-permute-start(bf16[256,768]{1,0:T(8,128)(2,1)S(1)} %fusion.6), channel_id=1, source_target_pairs={{0,2},{1,3},{2,0},{3,1},{4,6},{5,7},{6,4},{7,5},{8,10},{9,11},{10,... | collective-permute-start | bytes 1179656 | tf_op jit(solution)/shard_map/ppermute | solution.py:18
  158.6 22.2 %collective-permute-start.2 = (bf16[256,768]{1,0:T(8,128)(2,1)S(1)}, bf16[256,768]{1,0:T(8,128)(2,1)S(1)}, u32[]{:S(2)}, u32[]{:S(2)}) collective-permute-start(bf16[256,768]{1,0:T(8,128)(2,1)S(1)} %fusion.6), channel_id=1, source_target_pairs={{0,3},{1,2},{2,1},{3,0},{4,7},{5,6},{6,5},{7,4},{8,11},{9,10},{10,... | collective-permute-start | bytes 1179656 | tf_op jit(solution)/shard_map/ppermute | solution.py:18
  162.4 21.8 %collective-permute-start.3 = (bf16[16,1536]{1,0:T(8,128)(2,1)S(1)}, bf16[16,1536]{1,0:T(8,128)(2,1)S(1)}, u32[]{:S(2)}, u32[]{:S(2)}) collective-permute-start(bf16[16,1536]{1,0:T(8,128)(2,1)S(1)} %pad_maximum_fusion.3), channel_id=1, source_target_pairs={{0,4},{1,5},{2,6},{3,7},{4,0},{5,1},{6,2},{7,3},{8,12},{9,13},{10,... | collective-permute-start | bytes 147464 | tf_op jit(solution)/shard_map/ppermute | solution.py:18
  162.5 21.7 %collective-permute-start.4 = (bf16[16,1536]{1,0:T(8,128)(2,1)S(1)}, bf16[16,1536]{1,0:T(8,128)(2,1)S(1)}, u32[]{:S(2)}, u32[]{:S(2)}) collective-permute-start(bf16[16,1536]{1,0:T(8,128)(2,1)S(1)} %pad_maximum_fusion.3), channel_id=1, source_target_pairs={{0,5},{1,4},{2,7},{3,6},{4,1},{5,0},{6,3},{7,2},{8,13},{9,12},{10,... | collective-permute-start | bytes 147464 | tf_op jit(solution)/shard_map/ppermute | solution.py:18
  169.6 14.6 %collective-permute-start.5 = (bf16[16,1536]{1,0:T(8,128)(2,1)S(1)}, bf16[16,1536]{1,0:T(8,128)(2,1)S(1)}, u32[]{:S(2)}, u32[]{:S(2)}) collective-permute-start(bf16[16,1536]{1,0:T(8,128)(2,1)S(1)} %pad_maximum_fusion.3), channel_id=1, source_target_pairs={{0,6},{1,7},{2,4},{3,5},{4,2},{5,3},{6,0},{7,1},{8,14},{9,15},{10,... | collective-permute-start | bytes 147464 | tf_op jit(solution)/shard_map/ppermute | solution.py:18
  172.7 11.6 %collective-permute-start.6 = (bf16[16,1536]{1,0:T(8,128)(2,1)S(1)}, bf16[16,1536]{1,0:T(8,128)(2,1)S(1)}, u32[]{:S(2)}, u32[]{:S(2)}) collective-permute-start(bf16[16,1536]{1,0:T(8,128)(2,1)S(1)} %pad_maximum_fusion.3), channel_id=1, source_target_pairs={{0,7},{1,6},{2,5},{3,4},{4,3},{5,2},{6,1},{7,0},{8,15},{9,14},{10,... | collective-permute-start | bytes 147464 | tf_op jit(solution)/shard_map/ppermute | solution.py:18
  182.2 2.1 %copy-start.4 = (bf16[768,768]{1,0:T(8,128)(2,1)S(1)}, bf16[768,768]{1,0:T(8,128)(2,1)}, u32[]{:S(2)}) copy-start(bf16[768,768]{1,0:T(8,128)(2,1)} %o_ref.1) | copy-start | bytes 3538948
